TPU v7x, 32 devices: a whole 2x2x4 slice. The times are simulated.
32 devices in a mesh: dp: 8 (over y, x, core), seq: 4 (over z).
Axes of the slice: x: 2, y: 2, z: 4, core: 2. Of those that a mesh axis runs over, the one named last changes fastest.
Arguments:
- tokens: bfloat16 [32, 640, 1024], P('dp', 'seq'), may hold values from -6 to 6
- filled: int32 [32, 640], P('dp', 'seq'), may hold values from 0 to 1, as said below
- out_grad: bfloat16 [32, 640, 1024], P('dp', 'seq'), may hold values from -6 to 6
- norm1_gain: bfloat16 [1024], P('dp'), may hold values from 0.25 to 1.75
- norm1_bias: bfloat16 [1024], P('dp'), may hold values from -3 to 3
- qkv_weight: bfloat16 [1024, 3072], P('dp'), may hold values from -1 to 1
- qv_bias: bfloat16 [2048], P('dp'), may hold values from -3 to 3
- out_weight: bfloat16 [1024, 1024], P('dp'), may hold values from -1 to 1
- out_bias: bfloat16 [1024], P('dp'), may hold values from -3 to 3
- norm2_gain: bfloat16 [1024], P('dp'), may hold values from 0.25 to 1.75
- norm2_bias: bfloat16 [1024], P('dp'), may hold values from -3 to 3
- up_weight: bfloat16 [1024, 4096], P('dp'), may hold values from -0.1875 to 0.1875
- up_bias: bfloat16 [4096], P('dp'), may hold values from -3 to 3
- down_weight: bfloat16 [4096, 1024], P('dp'), may hold values from -0.1875 to 0.1875
- down_bias: bfloat16 [1024], P('dp'), may hold values from -3 to 3
- clip_threshold: int32 [], replicated, may hold values from 8 to 12
Outputs:
- block_out: bfloat16 [32, 640, 1024], P('dp', 'seq')
- tokens_grad: bfloat16 [32, 640, 1024], P('dp', 'seq')
- norm1_gain_grad: float32 [1024], P('dp')
- norm1_bias_grad: float32 [1024], P('dp')
- qkv_weight_grad: float32 [1024, 3072], P('dp')
- qv_bias_grad: float32 [2048], P('dp')
- out_weight_grad: float32 [1024, 1024], P('dp')
- out_bias_grad: float32 [1024], P('dp')
- norm2_gain_grad: float32 [1024], P('dp')
- norm2_bias_grad: float32 [1024], P('dp')
- up_weight_grad: float32 [1024, 4096], P('dp')
- up_bias_grad: float32 [4096], P('dp')
- down_weight_grad: float32 [4096, 1024], P('dp')
- down_bias_grad: float32 [1024], P('dp')
- clipped_qkv_weight: bfloat16 [1024, 3072], P('dp')
- clipped_qv_bias: bfloat16 [2048], P('dp')
- head_max: float32 [16], replicated
Inputs may be any that keep to these rules, and one draw needn't show every extreme that they name: `filled`: each image's flags are 1 on a leading run of at least 320 slots and 0 after it.
All inputs are finite; a program needn't handle non-finite values.
Results may differ from a plain program's by a relative error of at most 0.018.
Values may be sent and summed in bfloat16 or wider, within the bound.
A program may use at most 192 MiB of HBM per device.

v0:
```python
import jax
import jax.numpy as jnp
from jax import lax
from jax.sharding import PartitionSpec as P

H = 16
HD = 64


epsilon = 1e-06
very_negative = -1e30


def norm_apply(values, gain_vec, shift_vec):
    center = jnp.mean(values, axis=-1, keepdims=True)
    centered = values - center
    spread = jnp.mean(centered * centered, axis=-1, keepdims=True)
    return centered * lax.rsqrt(spread + epsilon) * gain_vec + shift_vec


def exact_gelu(values):
    return jax.nn.gelu(values, approximate=False)


def last_dot(left_op, right_op):
    return lax.dot_general(
        left_op, right_op, (((1,), (1,)), ((), ())), preferred_element_type=jnp.float32
    )


def first_dot(left_op, right_op):
    return lax.dot_general(
        left_op, right_op, (((0,), (0,)), ((), ())), preferred_element_type=jnp.float32
    )


def column_sum(values):
    return jnp.sum(values.astype(jnp.float32), axis=0)


def score_block(queries, keys_in, key_keep):
    raw_scores = jnp.einsum(
        "qhd,khd->hqk", queries, keys_in, preferred_element_type=jnp.float32
    ) * HD ** (-0.5)
    masked = jnp.where(key_keep[None, None, :], raw_scores, very_negative)
    return (raw_scores, masked)


def attend_forward(inputs):
    queries, keys_in, values_in, key_keep = inputs
    raw_scores, masked = score_block(queries, keys_in, key_keep)
    row_peak = jnp.max(masked, axis=-1, keepdims=True)
    exp_scores = jnp.exp(masked - row_peak)
    row_total = jnp.sum(exp_scores, axis=-1, keepdims=True)
    soft_probs = (exp_scores / row_total).astype(jnp.bfloat16)
    mixed_rows = jnp.einsum(
        "hqk,khd->qhd", soft_probs, values_in, preferred_element_type=jnp.float32
    )
    logsum = row_peak + jnp.log(row_total)
    pair_keep = key_keep[:, None] & key_keep[None, :]
    head_top = jnp.max(jnp.where(pair_keep[None], raw_scores, very_negative), axis=(1, 2))
    flat_rows = mixed_rows.astype(jnp.bfloat16).reshape(mixed_rows.shape[0], -1)
    return (flat_rows, logsum, head_top)


def attend_backward(inputs):
    queries, keys_in, values_in, key_keep, logsum, upstream = inputs
    raw_scores, masked = score_block(queries, keys_in, key_keep)
    soft_probs = jnp.exp(masked - logsum)
    probs_low = soft_probs.astype(jnp.bfloat16)
    value_grad = jnp.einsum("hqk,qhd->khd", probs_low, upstream, preferred_element_type=jnp.float32)
    prob_grad = jnp.einsum("qhd,khd->hqk", upstream, values_in, preferred_element_type=jnp.float32)
    inner_sum = jnp.sum(soft_probs * prob_grad, axis=-1, keepdims=True)
    score_grad = (soft_probs * (prob_grad - inner_sum)).astype(jnp.bfloat16)
    score_scale = HD ** (-0.5)
    query_grad = (
        jnp.einsum("hqk,khd->qhd", score_grad, keys_in, preferred_element_type=jnp.float32)
        * score_scale
    )
    key_grad = (
        jnp.einsum("hqk,qhd->khd", score_grad, queries, preferred_element_type=jnp.float32)
        * score_scale
    )
    stacked = jnp.stack([query_grad, key_grad, value_grad], axis=1)
    return stacked.astype(jnp.bfloat16).reshape(stacked.shape[0], 3, -1)


def local(
    tokens,
    filled,
    out_grad,
    norm1_gain,
    norm1_bias,
    qkv_weight,
    qv_bias,
    out_weight,
    out_bias,
    norm2_gain,
    norm2_bias,
    up_weight,
    up_bias,
    down_weight,
    down_bias,
    clip_threshold,
):
    gathered = (
        lax.all_gather(norm1_gain, "dp", axis=0, tiled=True),
        lax.all_gather(norm1_bias, "dp", axis=0, tiled=True),
        lax.all_gather(qkv_weight, "dp", axis=0, tiled=True),
        lax.all_gather(qv_bias, "dp", axis=0, tiled=True),
        lax.all_gather(out_weight, "dp", axis=0, tiled=True),
        lax.all_gather(out_bias, "dp", axis=0, tiled=True),
        lax.all_gather(norm2_gain, "dp", axis=0, tiled=True),
        lax.all_gather(norm2_bias, "dp", axis=0, tiled=True),
        lax.all_gather(up_weight, "dp", axis=0, tiled=True),
        lax.all_gather(up_bias, "dp", axis=0, tiled=True),
        lax.all_gather(down_weight, "dp", axis=0, tiled=True),
        lax.all_gather(down_bias, "dp", axis=0, tiled=True),
    )
    (
        gain_one,
        shift_one,
        w_qkv,
        b_qv,
        w_out,
        b_out,
        gain_two,
        shift_two,
        w_up,
        b_up,
        w_down,
        b_down,
    ) = gathered
    images, local_rows, model_width = tokens.shape
    groups = lax.axis_size("seq")
    group_width = model_width // groups
    local_heads = group_width // HD
    length = local_rows * groups
    row_count = images * local_rows
    tokens_flat = tokens.astype(jnp.float32).reshape(row_count, model_width)
    gain_one_f = gain_one.astype(jnp.float32)
    shift_one_f = shift_one.astype(jnp.float32)
    gain_two_f = gain_two.astype(jnp.float32)
    shift_two_f = shift_two.astype(jnp.float32)
    hidden_one = norm_apply(tokens_flat, gain_one_f, shift_one_f).astype(jnp.bfloat16)
    bias_float = b_qv.astype(jnp.float32)
    qkv_bias = jnp.concatenate(
        [bias_float[:model_width], jnp.zeros((model_width,), jnp.float32), bias_float[model_width:]]
    )
    projected = (jnp.dot(hidden_one, w_qkv, preferred_element_type=jnp.float32) + qkv_bias).astype(
        jnp.bfloat16
    )
    key_flags = lax.all_gather(filled, "seq", axis=1, tiled=True)
    keep_all = key_flags > 0
    by_heads = lax.all_to_all(
        projected.reshape(images, local_rows, 3, groups, group_width),
        "seq",
        split_axis=3,
        concat_axis=1,
        tiled=True,
    )
    by_heads = by_heads.reshape(images, length, 3, local_heads, HD)
    queries = by_heads[:, :, 0]
    keys_all = by_heads[:, :, 1]
    values_all = by_heads[:, :, 2]
    attended, logsums, tops = lax.map(attend_forward, (queries, keys_all, values_all, keep_all))
    local_peak = jnp.max(tops, axis=0)
    peak_vector = lax.dynamic_update_slice(
        jnp.full((H,), very_negative, jnp.float32),
        local_peak,
        (lax.axis_index("seq") * local_heads,),
    )
    head_max = lax.pmax(peak_vector, ("dp", "seq"))
    back_rows = lax.all_to_all(
        attended.reshape(images, groups, local_rows, group_width),
        "seq",
        split_axis=1,
        concat_axis=3,
        tiled=True,
    )
    attn_rows = back_rows.reshape(row_count, model_width)
    branch = jnp.dot(attn_rows, w_out, preferred_element_type=jnp.float32) + b_out.astype(
        jnp.float32
    )
    middle = tokens_flat + branch
    hidden_two = norm_apply(middle, gain_two_f, shift_two_f).astype(jnp.bfloat16)
    pre_act = jnp.dot(hidden_two, w_up, preferred_element_type=jnp.float32) + b_up.astype(
        jnp.float32
    )
    activated = exact_gelu(pre_act).astype(jnp.bfloat16)
    block_rows = middle + (
        jnp.dot(activated, w_down, preferred_element_type=jnp.float32) + b_down.astype(jnp.float32)
    )
    block_out = block_rows.astype(jnp.bfloat16).reshape(tokens.shape)
    gain_one_b, w_qkv_b, w_out_b, gain_two_b, w_up_b, w_down_b = (
        lax.all_gather(norm1_gain, "dp", axis=0, tiled=True),
        lax.all_gather(qkv_weight, "dp", axis=0, tiled=True),
        lax.all_gather(out_weight, "dp", axis=0, tiled=True),
        lax.all_gather(norm2_gain, "dp", axis=0, tiled=True),
        lax.all_gather(up_weight, "dp", axis=0, tiled=True),
        lax.all_gather(down_weight, "dp", axis=0, tiled=True),
    )
    upstream = out_grad.reshape(row_count, model_width)
    upstream_f = upstream.astype(jnp.float32)
    d_bias_down = jnp.sum(upstream_f, axis=0)
    d_down = first_dot(activated, upstream)
    act_grad = last_dot(upstream, w_down_b)
    gelu_out, gelu_pull = jax.vjp(exact_gelu, pre_act)
    pre_grad = gelu_pull(act_grad)[0].astype(jnp.bfloat16)
    d_bias_up = column_sum(pre_grad)
    d_up = first_dot(hidden_two, pre_grad)
    hidden_two_grad = last_dot(pre_grad, w_up_b)
    norm_out_two, pull_two = jax.vjp(
        norm_apply, middle, gain_two_b.astype(jnp.float32), shift_two_f
    )
    mid_norm_grad, d_gain_two, d_shift_two = pull_two(hidden_two_grad)
    middle_grad = upstream_f + mid_norm_grad
    branch_grad = middle_grad.astype(jnp.bfloat16)
    d_bias_out = column_sum(branch_grad)
    d_out = first_dot(attn_rows, branch_grad)
    attn_grad = last_dot(branch_grad, w_out_b).astype(jnp.bfloat16)
    grad_heads = lax.all_to_all(
        attn_grad.reshape(images, local_rows, groups, group_width),
        "seq",
        split_axis=2,
        concat_axis=1,
        tiled=True,
    )
    grad_heads = grad_heads.reshape(images, length, local_heads, HD)
    head_grads = lax.map(
        attend_backward, (queries, keys_all, values_all, keep_all, logsums, grad_heads)
    )
    token_grads = lax.all_to_all(
        head_grads.reshape(images, groups, local_rows, 3, group_width),
        "seq",
        split_axis=1,
        concat_axis=4,
        tiled=True,
    )
    token_grads = token_grads.reshape(row_count, 3 * model_width)
    d_qkv = first_dot(hidden_one, token_grads)
    bias_sums = column_sum(token_grads)
    d_bias_qv = jnp.concatenate([bias_sums[:model_width], bias_sums[2 * model_width :]])
    first_grad = last_dot(token_grads, w_qkv_b)
    norm_out_one, pull_one = jax.vjp(
        norm_apply, tokens_flat, gain_one_b.astype(jnp.float32), shift_one_f
    )
    in_norm_grad, d_gain_one, d_shift_one = pull_one(first_grad)
    tokens_grad = (middle_grad + in_norm_grad).astype(jnp.bfloat16).reshape(tokens.shape)
    terms = (
        d_gain_one,
        d_shift_one,
        d_qkv,
        d_bias_qv,
        d_out,
        d_bias_out,
        d_gain_two,
        d_shift_two,
        d_up,
        d_bias_up,
        d_down,
        d_bias_down,
    )
    data_shards = (
        lax.psum_scatter(
            terms[0].astype(jnp.bfloat16), "dp", scatter_dimension=0, tiled=True
        ).astype(jnp.float32),
        lax.psum_scatter(
            terms[1].astype(jnp.bfloat16), "dp", scatter_dimension=0, tiled=True
        ).astype(jnp.float32),
        lax.psum_scatter(
            terms[2].astype(jnp.bfloat16), "dp", scatter_dimension=0, tiled=True
        ).astype(jnp.float32),
        lax.psum_scatter(
            terms[3].astype(jnp.bfloat16), "dp", scatter_dimension=0, tiled=True
        ).astype(jnp.float32),
        lax.psum_scatter(
            terms[4].astype(jnp.bfloat16), "dp", scatter_dimension=0, tiled=True
        ).astype(jnp.float32),
        lax.psum_scatter(
            terms[5].astype(jnp.bfloat16), "dp", scatter_dimension=0, tiled=True
        ).astype(jnp.float32),
        lax.psum_scatter(
            terms[6].astype(jnp.bfloat16), "dp", scatter_dimension=0, tiled=True
        ).astype(jnp.float32),
        lax.psum_scatter(
            terms[7].astype(jnp.bfloat16), "dp", scatter_dimension=0, tiled=True
        ).astype(jnp.float32),
        lax.psum_scatter(
            terms[8].astype(jnp.bfloat16), "dp", scatter_dimension=0, tiled=True
        ).astype(jnp.float32),
        lax.psum_scatter(
            terms[9].astype(jnp.bfloat16), "dp", scatter_dimension=0, tiled=True
        ).astype(jnp.float32),
        lax.psum_scatter(
            terms[10].astype(jnp.bfloat16), "dp", scatter_dimension=0, tiled=True
        ).astype(jnp.float32),
        lax.psum_scatter(
            terms[11].astype(jnp.bfloat16), "dp", scatter_dimension=0, tiled=True
        ).astype(jnp.float32),
    )
    shards = (
        lax.psum(data_shards[0].astype(jnp.bfloat16), "seq").astype(jnp.float32),
        lax.psum(data_shards[1].astype(jnp.bfloat16), "seq").astype(jnp.float32),
        lax.psum(data_shards[2].astype(jnp.bfloat16), "seq").astype(jnp.float32),
        lax.psum(data_shards[3].astype(jnp.bfloat16), "seq").astype(jnp.float32),
        lax.psum(data_shards[4].astype(jnp.bfloat16), "seq").astype(jnp.float32),
        lax.psum(data_shards[5].astype(jnp.bfloat16), "seq").astype(jnp.float32),
        lax.psum(data_shards[6].astype(jnp.bfloat16), "seq").astype(jnp.float32),
        lax.psum(data_shards[7].astype(jnp.bfloat16), "seq").astype(jnp.float32),
        lax.psum(data_shards[8].astype(jnp.bfloat16), "seq").astype(jnp.float32),
        lax.psum(data_shards[9].astype(jnp.bfloat16), "seq").astype(jnp.float32),
        lax.psum(data_shards[10].astype(jnp.bfloat16), "seq").astype(jnp.float32),
        lax.psum(data_shards[11].astype(jnp.bfloat16), "seq").astype(jnp.float32),
    )
    limit = clip_threshold.astype(jnp.float32)
    root_factor = jnp.sqrt(limit / jnp.maximum(head_max, limit))
    head_cols = jnp.repeat(root_factor, HD)
    weight_scale = jnp.concatenate([head_cols, head_cols, jnp.ones((model_width,), jnp.float32)])
    clipped_weight = (qkv_weight.astype(jnp.float32) * weight_scale[None, :]).astype(jnp.bfloat16)
    bias_count = qv_bias.shape[0]
    bias_scale = jnp.concatenate([head_cols, jnp.ones((model_width,), jnp.float32)])
    shard_scale = lax.dynamic_slice_in_dim(
        bias_scale, lax.axis_index("dp") * bias_count, bias_count
    )
    clipped_bias = (qv_bias.astype(jnp.float32) * shard_scale).astype(jnp.bfloat16)
    return (
        block_out,
        tokens_grad,
        shards[0],
        shards[1],
        shards[2],
        shards[3],
        shards[4],
        shards[5],
        shards[6],
        shards[7],
        shards[8],
        shards[9],
        shards[10],
        shards[11],
        clipped_weight,
        clipped_bias,
        head_max,
    )


def solution(mesh):
    return jax.shard_map(
        local,
        mesh=mesh,
        in_specs=(
            P("dp", "seq", None),
            P("dp", "seq"),
            P("dp", "seq", None),
            P("dp"),
            P("dp"),
            P("dp", None),
            P("dp"),
            P("dp", None),
            P("dp"),
            P("dp"),
            P("dp"),
            P("dp", None),
            P("dp"),
            P("dp", None),
            P("dp"),
            P(),
        ),
        out_specs=(
            P("dp", "seq", None),
            P("dp", "seq", None),
            P("dp"),
            P("dp"),
            P("dp", None),
            P("dp"),
            P("dp", None),
            P("dp"),
            P("dp"),
            P("dp"),
            P("dp", None),
            P("dp"),
            P("dp", None),
            P("dp"),
            P("dp", None),
            P("dp"),
            P(),
        ),
        check_vma=False,
    )
```

profile of v0, /device:TPU:0, one launch (start us, length us, event | category | flops | bytes accessed | tf_op | source)
XLA Modules:
  0.0 803.5 jit_solution(5568353933308388383)
XLA Ops:
  9.4 10.3 %all-gather.1 = bf16[8,1,128]{2,1,0:T(2,128)(2,1)S(1)} all-gather(bf16[1,1,128]{2,1,0:T(2,128)(2,1)} %bitcast.245), channel_id=1, replica_groups=mesh['dp'=8,'seq'=4] {'dp'}, dimensions={0}, use_global_device_ids=true | all-gather | bytes 2304 | tf_op jit(solution)/shard_map/all_gather | solution.py:108
  19.7 8.6 %all-gather = bf16[8,1,128]{2,1,0:T(2,128)(2,1)S(1)} all-gather(bf16[1,1,128]{2,1,0:T(2,128)(2,1)} %bitcast.246), channel_id=1, replica_groups=mesh['dp'=8,'seq'=4] {'dp'}, dimensions={0}, use_global_device_ids=true | all-gather | bytes 2304 | tf_op jit(solution)/shard_map/all_gather | solution.py:107
  31.3 8.0 all-gather.2
  39.9 18.3 %all-gather.14.cloned.1.call-done = bf16[1024,3072]{1,0:T(8,128)(2,1)} async-done(((bf16[128,3072]{1,0:T(8,128)(2,1)}), bf16[1024,3072]{1,0:T(8,128)(2,1)}) %all-gather.14.cloned.1.call-update) | async-done | bytes 6291472 | tf_op jit(solution)/shard_map/all_gather | solution.py:109
  58.2 8.5 %add_convert_fusion.1 = bf16[640,3072]{1,0:T(8,128)(2,1)} fusion(bf16[640,1024]{1,0:T(8,128)(2,1)S(1)} %fusion.60, bf16[1024,3072]{1,0:T(8,128)(2,1)} %all-gather.14.cloned.1.call-done, f32[3072]{0:T(1024)S(1)} %pad_maximum_fusion.1), kind=kOutput, calls=%fused_computation.77 | convolution fusion | flops 4030464000 | bytes 11546624 | tf_op jit(solution)/shard_map/dot_general | solution.py:150
  66.7 8.1 %reshape.301 = bf16[4,160,3,4,256]{4,3,2,1,0:T(4,128)(2,1)} reshape(bf16[640,3072]{1,0:T(8,128)(2,1)} %add_convert_fusion.1) | data formatting | bytes 7864320 | tf_op jit(solution)/shard_map/reshape | solution.py:156
  74.8 4.7 copy.99
  79.5 4.9 all-to-all-start
  85.0 93.0 %all-gather.3 = s32[4,160,4]{1,2,0:T(4,128)S(1)} all-gather(s32[1,160,4]{1,2,0:T(4,128)S(1)} %bitcast.240), channel_id=1, replica_groups=mesh['dp'=8,'seq'=4] {'seq'}, dimensions={0}, use_global_device_ids=true | all-gather | bytes 12800 | tf_op jit(solution)/shard_map/all_gather | solution.py:153
  178.1 10.0 %copy.100 = bf16[4,4,160,3,1,256]{2,1,5,3,0,4:T(4,128)(2,1)} copy(bf16[4,4,160,3,1,256]{5,2,3,0,1,4:T(8,128)(2,1)} %bitcast.26) | data formatting | bytes 7864320 | tf_op jit(solution)/shard_map/all_to_all | solution.py:155
  188.1 11.0 %reshape.302 = bf16[4,640,3,4,64]{1,4,3,2,0:T(8,128)(2,1)} reshape(bf16[4,4,160,3,1,256]{2,1,5,3,0,4:T(4,128)(2,1)} %copy.100) | data formatting | bytes 7864320 | tf_op jit(solution)/shard_map/reshape | solution.py:162
  199.1 4.0 slice_bitcast_fusion
  203.2 46.8 %while.24 = (s32[]{:T(128)}, bf16[4,640,256]{2,1,0:T(8,128)(2,1)}, f32[4,4,640,1]{2,1,3,0:T(4,128)}, f32[4,4]{1,0:T(4,128)}, bf16[4,640,4,64]{1,3,2,0:T(8,128)(2...) while((s32[]{:T(128)}, bf16[4,640,256]{2,1,0:T(8,128)(2,1)}, ...), condition=%wide.region_6.7_spmd, body=%wide.region_2.6_spmd.sunk | while | flops 442938880 | bytes 23188784 | solution.py:166
  203.2 2.5 select_reduce_fusion.4
  206.0 3.2 select_reduce_fusion.5
  209.2 2.9 fusion.121
  214.9 2.5 select_reduce_fusion.4
  217.7 3.2 select_reduce_fusion.5
  220.9 2.9 fusion.121
  229.4 3.2 select_reduce_fusion.5
  232.6 2.9 fusion.121
  241.1 3.2 select_reduce_fusion.5
  244.3 2.9 fusion.121
  250.0 3.0 copy.103
  253.0 4.3 all-to-all-start.1
  257.4 8.7 %all-gather.4 = bf16[8,1,128]{2,1,0:T(2,128)(2,1)S(1)} all-gather(bf16[1,1,128]{2,1,0:T(2,128)(2,1)S(1)} %bitcast.247), channel_id=1, replica_groups=mesh['dp'=8,'seq'=4] {'dp'}, dimensions={0}, use_global_device_ids=true | all-gather | bytes 2304 | tf_op jit(solution)/shard_map/all_gather | solution.py:112
  266.1 7.8 all-gather.6
  273.9 8.7 %all-gather.5 = bf16[8,1,128]{2,1,0:T(2,128)(2,1)S(1)} all-gather(bf16[1,1,128]{2,1,0:T(2,128)(2,1)S(1)} %bitcast.249), channel_id=1, replica_groups=mesh['dp'=8,'seq'=4] {'dp'}, dimensions={0}, use_global_device_ids=true | all-gather | bytes 2304 | tf_op jit(solution)/shard_map/all_gather | solution.py:113
  282.6 8.2 %all-gather.7 = bf16[8,1,512]{2,1,0:T(2,128)(2,1)S(1)} all-gather(bf16[1,1,512]{2,1,0:T(2,128)(2,1)S(1)} %reshape.327), channel_id=1, replica_groups=mesh['dp'=8,'seq'=4] {'dp'}, dimensions={0}, use_global_device_ids=true | all-gather | bytes 9216 | tf_op jit(solution)/shard_map/all_gather | solution.py:116
  293.5 3.2 fusion.81
  298.6 11.5 %fusion.73 = f32[640,4096]{1,0:T(8,128)} fusion(bf16[1024,4096]{1,0:T(8,128)(2,1)} %all-gather.18.cloned.1.call-done, f32[640,1024]{1,0:T(8,128)} %copy-done.7, f32[1024]{0:T(1024)S(1)} %bitcast.242, f32[1024]{0:T(1024)S(1)} %bitcast.230, f32[640]{0:T(1024)S(1)} %fusion.68, f32[640]{0:T(1024)S(1)} %broadcast_multiply_fusion), kind=kOutput, calls=%fused_computation.138 | convolution fusion | flops 5371985920 | bytes 21509120 | tf_op jit(solution)/shard_map/dot_general | solution.py:187
  310.2 34.2 %fusion.75 = (bf16[4096]{0:T(1024)(128)(2,1)}, bf16[640,4096]{1,0:T(8,128)(2,1)S(1)}, f32[640,4096]{1,0:T(8,128)}) fusion(f32[640,4096]{1,0:T(8,128)} %fusion.73, f32[4096]{0:T(1024)S(1)} %bitcast.225, bf16[640,1024]{1,0:T(8,128)(2,1)S(1)} %bitcast.207, bf16[4096,1024]{1,0:T(8,128)(2,1)} %all-gather.20.cloned.1.call-done), kind=kOutput, calls=%fused_computation.140 | convolution fusion | flops 5562691584 | bytes 35938304 | tf_op jit(solution)/shard_map/dot_general | solution.py:26
  344.4 6.6 multiply_reduce_fusion.1
  355.5 3.2 convolution_convert_fusion.3
  358.8 12.0 %convolution_convert_fusion = bf16[1024,4096]{1,0:T(8,128)(2,1)} fusion(bf16[640,4096]{1,0:T(8,128)(2,1)} %copy-done.52, f32[640,1024]{1,0:T(8,128)} %copy-done.7, f32[1024]{0:T(1024)S(1)} %bitcast.243, f32[1024]{0:T(1024)S(1)} %bitcast.233, f32[640]{0:T(1024)S(1)} %fusion.68, f32[640]{0:T(1024)S(1)} %broadcast_multiply_fusion), kind=kOutput, calls=%fused_computation.78 | convolution fusion | flops 5376180224 | bytes 16266240 | tf_op jit(solution)/shard_map/dot_general | solution.py:32
  372.2 4.2 convolution_convert_fusion.4
  376.4 2.9 reshape.307
  380.5 5.0 all-to-all-start.2
  385.5 8.1 %multiply_convert_fusion.1 = bf16[640,4096]{1,0:T(8,128)(2,1)S(1)} fusion(f32[640,4096]{1,0:T(8,128)} %get-tuple-element.172, f32[640,4096]{1,0:T(8,128)} %fusion.73, f32[4096]{0:T(1024)S(1)} %bitcast.226), kind=kLoop, calls=%fused_computation.63 | loop fusion | flops 10485760 | bytes 26230784 | tf_op jit(solution)/shard_map/convert_element_type | solution.py:190
  395.8 9.0 %convolution_convert_fusion.1 = bf16[4096,1024]{1,0:T(8,128)(2,1)} fusion(bf16[640,4096]{1,0:T(8,128)(2,1)S(1)} %multiply_convert_fusion.1, bf16[640,1024]{1,0:T(8,128)(2,1)S(1)} %bitcast.208), kind=kOutput, calls=%fused_computation.79 | convolution fusion | flops 5372903424 | bytes 14942208 | tf_op jit(solution)/shard_map/dot_general | solution.py:32
  404.9 12.5 %all-to-all-done.2 = bf16[4,160,4,256]{3,1,0,2:T(8,128)(2,1)S(1)} async-done(((bf16[4,160,4,256]{3,1,0,2:T(8,128)(2,1)}), bf16[4,160,4,256]{3,1,0,2:T(8,128)(2,1)S(1)}, u32[]{:S(2)}, u32[]{:S(2)}) %all-to-all-start.2) | async-done | bytes 1310752 | tf_op jit(solution)/shard_map/all_to_all | solution.py:222
  418.4 3.1 copy.106
  423.7 58.8 %while.25 = (s32[]{:T(128)}, bf16[4,640,3,256]{3,1,2,0:T(8,128)(2,1)}, bf16[4,640,4,64]{1,3,2,0:T(8,128)(2,1)S(1)}, pred[4,640]{1,0:T(4,128)(4,1)S(1)}, bf16[4,6...) while((s32[]{:T(128)}, ...), condition=%wide.region_13.14_spmd, body=%wide.region_11.13_spmd.sunk | while | flops 1074951680 | bytes 63647768 | solution.py:230
  428.5 3.3 multiply_reduce_fusion.5
  443.2 3.2 multiply_reduce_fusion.5
  457.8 3.2 multiply_reduce_fusion.5
  472.4 3.2 multiply_reduce_fusion.5
  482.4 4.5 copy.108
  486.9 5.1 all-to-all-start.3
  492.7 86.4 %all-to-all-done.3 = bf16[4,4,160,3,256]{4,2,3,0,1:T(8,128)(2,1)} async-done(((bf16[4,4,160,3,256]{4,2,3,0,1:T(8,128)(2,1)}), bf16[4,4,160,3,256]{4,2,3,0,1:T(8,128)(2,1)}, u32[]{:S(2)}, u32[]{:S(2)}) %all-to-all-start.3) | async-done | bytes 3932192 | tf_op jit(solution)/shard_map/all_to_all | solution.py:233
  579.1 7.0 copy.109
  586.1 8.0 %reshape.310 = bf16[640,3072]{1,0:T(8,128)(2,1)} reshape(bf16[4,1,160,3,4,256]{5,4,3,2,0,1:T(4,128)(2,1)} %copy.109) | data formatting | bytes 7864320 | tf_op jit(solution)/shard_map/reshape | solution.py:240
  594.1 9.2 %convolution_convert_fusion.2 = bf16[1024,3072]{1,0:T(8,128)(2,1)} fusion(bf16[640,1024]{1,0:T(8,128)(2,1)S(1)} %bitcast.214, bf16[640,3072]{1,0:T(8,128)(2,1)} %reshape.310), kind=kOutput, calls=%fused_computation.80 | convolution fusion | flops 4029677568 | bytes 11534336 | tf_op jit(solution)/shard_map/dot_general | solution.py:32
  604.0 8.9 %all-gather.8 = bf16[8,1,128]{2,1,0:T(2,128)(2,1)S(1)} all-gather(bf16[1,1,128]{2,1,0:T(2,128)(2,1)S(1)} %bitcast.250), channel_id=1, replica_groups=mesh['dp'=8,'seq'=4] {'dp'}, dimensions={0}, use_global_device_ids=true | all-gather | bytes 2304 | tf_op jit(solution)/shard_map/all_gather | solution.py:118
  616.6 37.1 %pmax.7 = f32[16]{0:T(128)S(1)} all-reduce(f32[16]{0:T(128)S(1)} %dynamic_update_slice.19), channel_id=1, replica_groups=mesh['dp'=8,'seq'=4] {'dp','seq'}, use_global_device_ids=true, to_apply=%region_49.50 | all-reduce | flops 16 | bytes 128 | tf_op jit(solution)/shard_map/pmax | solution.py:173
  655.5 8.3 %reduce-scatter.5.cloned.1.call-done = bf16[128,3072]{1,0:T(8,128)(2,1)} async-done(((bf16[1024,3072]{1,0:T(8,128)(2,1)}), bf16[128,3072]{1,0:T(8,128)(2,1)}) %reduce-scatter.5.cloned.1.call-update) | async-done | bytes 786448 | tf_op jit(solution)/shard_map/reduce_scatter | solution.py:271
  663.8 10.8 %add_convert_fusion.3 = bf16[640,1024]{1,0:T(8,128)(2,1)} fusion(f32[640,1024]{1,0:T(8,128)} %copy-done.7, bf16[640,4096]{1,0:T(8,128)(2,1)} %copy-done.12, bf16[4096,1024]{1,0:T(8,128)(2,1)} %all-gather.20.cloned.1.call-done, f32[1024]{0:T(1024)S(1)} %bitcast.241), kind=kOutput, calls=%fused_computation.106 | convolution fusion | flops 5370675200 | bytes 17567744 | tf_op jit(solution)/shard_map/dot_general | solution.py:192
  674.6 2.8 bitcast_reduce_fusion
  677.9 6.7 fusion.74
  687.4 24.9 %all-reduce.9 = (bf16[1024]{0:T(1024)(128)(2,1)S(1)}, bf16[1024]{0:T(1024)(128)(2,1)S(1)}, bf16[2048]{0:T(1024)(128)(2,1)S(1)}, bf16[1024]{0:T(1024)(128)(2,1)S(...) all-reduce(bf16[1024]{0:T(1024)(128)(2,1)S(1)} %get-tuple-element.1, ...), channel_id=2, replica_groups=mesh['dp'=8,'seq'=4] {'dp'}, use_global_device_ids=true, to_apply=%region_17.18.clone | all-reduce | flops 12288 | bytes 49152
  712.9 12.5 %all-reduce.10 = (bf16[128]{0:T(256)(128)(2,1)S(1)}, bf16[128]{0:T(256)(128)(2,1)S(1)}, bf16[256]{0:T(256)(128)(2,1)S(1)}, bf16[128]{0:T(256)(128)(2,1)S(1)}, bf...) all-reduce(bf16[128]{0:T(256)(128)(2,1)S(1)} %dynamic-slice.1, ...), channel_id=1, replica_groups=mesh['dp'=8,'seq'=4] {'seq'}, use_global_device_ids=true, to_apply=%region_18.19 | all-reduce | flops 1536 | bytes 6144 | tf_op jit(solution)/shard_map/psum | solution.py:303
  729.6 4.0 add_convert_fusion.2
  733.6 55.5 %all-reduce.14.cloned.1.call-done = (bf16[128,3072]{1,0:T(8,128)(2,1)}, bf16[128,1024]{1,0:T(8,128)(2,1)}, bf16[128,4096]{1,0:T(8,128)(2,1)}, bf16[512,1024]{1,0:T(8,128)(2,1)}) async-done(((bf16[128,3072]{1,0:T(8,128)(2,1)}, bf16[128,1024]{1,0:T(8,128)(2,1)}, bf16[128,4096]{1,0:T(8,128)(2,1)}, bf16[512,1024]{1,0:T(8,128)(2,1)}), (bf16[128,3072]{1,0:T(8,128)(2,1)}, bf16[128,1024]{1,0:T(8,128)(2,1)}, ...) | async-done | bytes 3145744 | tf_op jit(solution)/shard_map/psum | solution.py:305
  789.1 2.6 convert_element_type.222
  (281 shorter events, 103.4 us)
Async XLA Ops:
  7.2 22.8 %copy-start = (bf16[4,160,1024]{2,1,0:T(8,128)(2,1)S(1)}, bf16[4,160,1024]{2,1,0:T(8,128)(2,1)}, u32[]{:S(2)}) copy-start(bf16[4,160,1024]{2,1,0:T(8,128)(2,1)} %param.20) | copy-start | bytes 3932164
  7.2 24.0 %copy-start.47 = (bf16[256]{0:T(256)(128)(2,1)S(1)}, bf16[256]{0:T(256)(128)(2,1)}, u32[]{:S(2)}) copy-start(bf16[256]{0:T(256)(128)(2,1)} %param.26) | copy-start | bytes 1540
  7.2 51.0 %all-gather.14.cloned.1.call-start = ((), (), s32[]{:S(2)}) async-start(), calls=%async_computation.8 | async-start | bytes 7077888 | tf_op jit(solution)/shard_map/all_gather | solution.py:109
  7.9 285.5 %all-gather.16.cloned.1.call-start = ((), (), s32[]{:S(2)}) async-start(), calls=%async_computation.9 | async-start | bytes 2359296 | tf_op jit(solution)/shard_map/all_gather | solution.py:111
  8.7 289.9 %all-gather.18.cloned.1.call-start = ((), (), s32[]{:S(2)}) async-start(), calls=%async_computation.10 | async-start | bytes 9437184 | tf_op jit(solution)/shard_map/all_gather | solution.py:115
  19.7 46.9 %copy-start.29 = (f32[8,1,128]{2,1,0:T(1,128)}, f32[8,1,128]{2,1,0:T(1,128)S(1)}, u32[]{:S(2)}) copy-start(f32[8,1,128]{2,1,0:T(1,128)S(1)} %convert_element_type.244) | copy-start | bytes 12292
  28.4 38.3 %copy-start.21 = (f32[8,1,128]{2,1,0:T(1,128)}, f32[8,1,128]{2,1,0:T(1,128)S(1)}, u32[]{:S(2)}) copy-start(f32[8,1,128]{2,1,0:T(1,128)S(1)} %convert_element_type.243) | copy-start | bytes 12292
  29.9 9.4 %copy-start.23 = (f32[4,160]{1,0:T(4,128)}, f32[4,160]{1,0:T(4,128)S(1)}, u32[]{:S(2)}) copy-start(f32[4,160]{1,0:T(4,128)S(1)} %broadcast_multiply_fusion.1) | copy-start | bytes 7684
  30.0 36.6 %copy-start.25 = (f32[640]{0:T(1024)}, f32[640]{0:T(1024)S(1)}, u32[]{:S(2)}) copy-start(f32[640]{0:T(1024)S(1)} %div.57) | copy-start | bytes 7684
  31.2 8.1 %copy-start.31 = (f32[640]{0:T(1024)}, f32[640]{0:T(1024)S(1)}, u32[]{:S(2)}) copy-start(f32[640]{0:T(1024)S(1)} %add.169) | copy-start | bytes 7684
  31.3 8.1 %copy-start.27 = (f32[640]{0:T(1024)}, f32[640]{0:T(1024)S(1)}, u32[]{:S(2)}) copy-start(f32[640]{0:T(1024)S(1)} %rsqrt.25) | copy-start | bytes 7684
  79.5 5.6 copy-start.38
  79.5 98.7 %all-to-all-start = ((bf16[4,160,3,4,256]{4,1,2,0,3:T(8,128)(2,1)}), bf16[4,160,3,4,256]{4,1,2,0,3:T(8,128)(2,1)}, u32[]{:S(2)}, u32[]{:S(2)}) async-start(bf16[4,160,3,4,256]{4,1,2,0,3:T(8,128)(2,1)} %copy.99), calls=%async_computation | async-start | bytes 7864320 | tf_op jit(solution)/shard_map/all_to_all | solution.py:155
  84.4 225.7 %all-gather.20.cloned.1.call-start = ((), (), s32[]{:S(2)}) async-start(), calls=%async_computation.11 | async-start | bytes 9437184 | tf_op jit(solution)/shard_map/all_gather | solution.py:117
  250.0 43.2 %copy-start.2 = (bf16[4,640,4,64]{1,3,2,0:T(8,128)(2,1)}, bf16[4,640,4,64]{1,3,2,0:T(8,128)(2,1)S(1)}, u32[]{:S(2)}) copy-start(bf16[4,640,4,64]{1,3,2,0:T(8,128)(2,1)S(1)} %get-tuple-element.375) | copy-start | bytes 3932164
  250.0 43.2 %copy-start.19 = (pred[4,640]{1,0:T(4,128)(4,1)}, pred[4,640]{1,0:T(4,128)(4,1)S(1)}, u32[]{:S(2)}) copy-start(pred[4,640]{1,0:T(4,128)(4,1)S(1)} %get-tuple-element.411) | copy-start | bytes 7684
  250.0 7.4 copy-start.43
  250.0 16.1 %copy-start.44 = (bf16[128]{0:T(256)(128)(2,1)S(1)}, bf16[128]{0:T(256)(128)(2,1)}, u32[]{:S(2)}) copy-start(bf16[128]{0:T(256)(128)(2,1)} %param.30) | copy-start | bytes 772
  250.0 23.9 %copy-start.45 = (bf16[128]{0:T(256)(128)(2,1)S(1)}, bf16[128]{0:T(256)(128)(2,1)}, u32[]{:S(2)}) copy-start(bf16[128]{0:T(256)(128)(2,1)} %param.29) | copy-start | bytes 772
  250.0 32.5 %copy-start.42 = (bf16[512]{0:T(512)(128)(2,1)S(1)}, bf16[512]{0:T(512)(128)(2,1)}, u32[]{:S(2)}) copy-start(bf16[512]{0:T(512)(128)(2,1)} %param.32) | copy-start | bytes 3076
  253.0 37.8 %all-to-all-start.1 = ((bf16[4,4,160,256]{3,2,0,1:T(8,128)(2,1)}), bf16[4,4,160,256]{3,2,0,1:T(8,128)(2,1)}, u32[]{:S(2)}, u32[]{:S(2)}) async-start(bf16[4,4,160,256]{3,2,0,1:T(8,128)(2,1)} %copy.103), calls=%async_computation.1 | async-start | bytes 2621440 | tf_op jit(solution)/shard_map/all_to_all | solution.py:174
  257.3 398.2 %reduce-scatter.7.cloned.1.call-start = ((), (), s32[]{:S(2)}) async-start(), calls=%async_computation.13 | async-start | bytes 2359296 | tf_op jit(solution)/shard_map/reduce_scatter | solution.py:277
  298.6 11.5 %copy-start.5 = (bf16[4,160,1024]{2,1,0:T(8,128)(2,1)S(1)}, bf16[4,160,1024]{2,1,0:T(8,128)(2,1)}, u32[]{:S(2)}) copy-start(bf16[4,160,1024]{2,1,0:T(8,128)(2,1)} %param.22) | copy-start | bytes 3932164
  310.2 34.3 %copy-start.8 = (f32[640,1024]{1,0:T(8,128)S(1)}, f32[640,1024]{1,0:T(8,128)}, u32[]{:S(2)}) copy-start(f32[640,1024]{1,0:T(8,128)} %copy-done.7) | copy-start | bytes 7864324
  310.2 34.3 %copy-start.49 = (bf16[1024,4096]{1,0:T(8,128)(2,1)S(1)}, bf16[1024,4096]{1,0:T(8,128)(2,1)}, u32[]{:S(2)}) copy-start(bf16[1024,4096]{1,0:T(8,128)(2,1)} %all-gather.18.cloned.1.call-done) | copy-start | bytes 25165828
  344.4 6.6 copy-start.52
  351.9 1.6 copy-start.4
  351.9 6.8 copy-start.33
  358.7 296.7 %reduce-scatter.9.cloned.1.call-start = ((), (), s32[]{:S(2)}) async-start(), calls=%async_computation.14 | async-start | bytes 9437184 | tf_op jit(solution)/shard_map/reduce_scatter | solution.py:289
  380.5 36.8 %all-to-all-start.2 = ((bf16[4,160,4,256]{3,1,0,2:T(8,128)(2,1)}), bf16[4,160,4,256]{3,1,0,2:T(8,128)(2,1)S(1)}, u32[]{:S(2)}, u32[]{:S(2)}) async-start(bf16[4,160,4,256]{3,1,0,2:T(8,128)(2,1)} %copy.105), calls=%async_computation.2 | async-start | bytes 2621440 | tf_op jit(solution)/shard_map/all_to_all | solution.py:222
  385.5 269.9 %reduce-scatter.11.cloned.1.call-start = ((), (), s32[]{:S(2)}) async-start(), calls=%async_computation.15 | async-start | bytes 9437184 | tf_op jit(solution)/shard_map/reduce_scatter | solution.py:295
  393.6 2.3 copy-start.12
  418.4 5.2 copy-start.3
  418.4 5.2 copy-start.20
  423.9 2.9 copy-start.10
  438.6 2.9 copy-start.10
  453.2 2.9 copy-start.10
  467.8 2.9 copy-start.10
  486.9 5.2 copy-start.1
  486.9 5.2 copy-start.22
  486.9 5.2 copy-start.24
  486.9 5.2 copy-start.30
  486.9 5.2 copy-start.35
  486.9 92.2 %all-to-all-start.3 = ((bf16[4,4,160,3,256]{4,2,3,0,1:T(8,128)(2,1)}), bf16[4,4,160,3,256]{4,2,3,0,1:T(8,128)(2,1)}, u32[]{:S(2)}, u32[]{:S(2)}) async-start(bf16[4,4,160,3,256]{4,2,3,0,1:T(8,128)(2,1)} %copy.108), calls=%async_computation.3 | async-start | bytes 7864320 | tf_op jit(solution)/shard_map/all_to_all | solution.py:233
  492.0 171.8 %reduce-scatter.5.cloned.1.call-start = ((), (), s32[]{:S(2)}) async-start(), calls=%async_computation.12 | async-start | bytes 7077888 | tf_op jit(solution)/shard_map/reduce_scatter | solution.py:271
  603.3 9.5 %copy-start.6 = (bf16[4,160,1024]{2,1,0:T(8,128)(2,1)S(1)}, bf16[4,160,1024]{2,1,0:T(8,128)(2,1)}, u32[]{:S(2)}) copy-start(bf16[4,160,1024]{2,1,0:T(8,128)(2,1)} %param.22) | copy-start | bytes 3932164
  603.3 9.8 %copy-start.50 = (u32[32]{0:T(128)S(1)}, u32[32]{0:T(128)}, u32[]{:S(2)}) copy-start(u32[32]{0:T(128)} %constant.165) | copy-start | bytes 388
  603.3 13.0 %copy-start.41 = (f32[4,4]{1,0:T(4,128)S(1)}, f32[4,4]{1,0:T(4,128)}, u32[]{:S(2)}) copy-start(f32[4,4]{1,0:T(4,128)} %get-tuple-element.106) | copy-start | bytes 196
  603.3 50.5 %copy-start.48 = (bf16[256]{0:T(256)(128)(2,1)S(1)}, bf16[256]{0:T(256)(128)(2,1)}, u32[]{:S(2)}) copy-start(bf16[256]{0:T(256)(128)(2,1)} %param.26) | copy-start | bytes 1540
  603.4 51.1 %copy-start.14 = (bf16[128,3072]{1,0:T(8,128)(2,1)S(1)}, bf16[128,3072]{1,0:T(8,128)(2,1)}, u32[]{:S(2)}) copy-start(bf16[128,3072]{1,0:T(8,128)(2,1)} %param.25) | copy-start | bytes 2359300
  603.4 185.7 %all-reduce.14.cloned.1.call-start = ((), (), s32[]{:S(2)}) async-start(), calls=%async_computation.16 | async-start | bytes 6291456 | tf_op jit(solution)/shard_map/psum | solution.py:305
  653.7 21.0 %copy-start.51 = (f32[16]{0:T(128)}, f32[16]{0:T(128)S(1)}, u32[]{:S(2)}) copy-start(f32[16]{0:T(128)S(1)} %pmax.7) | copy-start | bytes 196
  674.6 3.3 copy-start.13
  674.6 3.3 copy-start.26
  677.9 6.7 copy-start.32
  677.9 8.2 %copy-start.28 = (f32[640]{0:T(1024)S(1)}, f32[640]{0:T(1024)}, u32[]{:S(2)}) copy-start(f32[640]{0:T(1024)} %copy-done.27) | copy-start | bytes 7684
  684.6 1.5 copy-start.9
  684.6 2.7 copy-start.36
  684.6 2.7 copy-start.37
  684.6 2.7 copy-start.39
  684.6 2.7 copy-start.40
  684.6 45.0 %copy-start.34 = (f32[640]{0:T(1024)S(1)}, f32[640]{0:T(1024)}, u32[]{:S(2)}) copy-start(f32[640]{0:T(1024)} %copy-done.33) | copy-start | bytes 7684
  789.1 4.4 copy-start.18
  789.1 5.9 copy-start.17
  (5 other events, 5.6 us)
Sparse Core Ops, SparseCore 0:
  9.9 48.2 all-gather.13
  60.1 27.8 all-gather.15
  89.9 54.3 all-gather.17
  146.1 54.3 all-gather.19
  358.8 41.6 reduce-scatter.6
  404.2 71.2 reduce-scatter.8
  479.0 71.2 reduce-scatter.10
  603.5 60.2 reduce-scatter.4
  666.4 122.6 all-reduce.13
where the time goes:
time: 811 us; the launch traced here: 804 us
  blocking collectives  237 us (29%)
  waiting for transfers between devices  184 us (23%)
  matrix products  180 us (22%)
  local copies, waits for them, and re-layouts  104 us (13%)
  other arithmetic  61.1 us (8%)
  starting transfers between devices  19.6 us (2%)
  between operations  17.6 us (2%)
    all_gather x1, blocking collectives, local(): key_flags = lax.all_gather(filled, 'seq', axis=1, tiled=True)  93 us
    all_to_all x1, waiting for transfers between devices, local(): lax.all_to_all(head_grads.reshape(images, groups, local_rows, 3, group_wi...  86.4 us
    psum x1, waiting for transfers between devices, local(): lax.psum(data_shards[2].astype(jnp.bfloat16), 'seq').astype(jnp.float32)  55.5 us
    dot_general x4, matrix products, last_dot(): lax.dot_general(left_op, right_op, (((1,), (1,)), ((), ())), preferred_el...  51.7 us
    pmax x1, blocking collectives, local(): head_max = lax.pmax(peak_vector, ('dp', 'seq'))  37.1 us
    dot_general x4, matrix products, first_dot(): lax.dot_general(left_op, right_op, (((0,), (0,)), ((), ())), preferred_el...  33.4 us
    unnamed x1, blocking collectives  24.9 us
    dot_general x8, matrix products, score_block(): jnp.einsum('qhd,khd->hqk', queries, keys_in, preferred_element_type=jnp.f...  18.6 us
  transfers between devices with their start and end apart: 13, of which 5 were waited for; matrix products, arithmetic and copies ran while one was open for 35% of the time, Pallas kernels for 0%

commit v1 on v0

--- a/solution.py
+++ b/solution.py
@@ -85,7 +85,7 @@
     return stacked.astype(jnp.bfloat16).reshape(stacked.shape[0], 3, -1)
 
 
-def local(
+def by_head_local(
     tokens,
     filled,
     out_grad,
@@ -345,6 +345,171 @@
     )
 
 
+def gather_small(pieces):
+    sizes = [piece.shape[0] for piece in pieces]
+    packed = jnp.concatenate(pieces)
+    everyone = lax.all_gather(packed, "dp", axis=0, tiled=False)
+    outs, start = [], 0
+    for size in sizes:
+        outs.append(everyone[:, start : start + size].reshape(-1))
+        start += size
+    return outs
+
+
+def by_image_local(
+    tokens,
+    filled,
+    out_grad,
+    norm1_gain,
+    norm1_bias,
+    qkv_weight,
+    qv_bias,
+    out_weight,
+    out_bias,
+    norm2_gain,
+    norm2_bias,
+    up_weight,
+    up_bias,
+    down_weight,
+    down_bias,
+    clip_threshold,
+):
+    images, local_rows, model_width = tokens.shape
+    length = local_rows * images
+    w_qkv = lax.all_gather(qkv_weight, "dp", axis=0, tiled=True)
+    small = gather_small(
+        [norm1_gain, norm1_bias, qv_bias, out_bias, norm2_gain, norm2_bias, up_bias, down_bias]
+    )
+    gain_one, shift_one, b_qv, b_out, gain_two, shift_two, b_up, b_down = [
+        piece.astype(jnp.float32) for piece in small
+    ]
+    w_out = lax.all_gather(out_weight, "dp", axis=0, tiled=True)
+    w_up = lax.all_gather(up_weight, "dp", axis=0, tiled=True)
+    w_down = lax.all_gather(down_weight, "dp", axis=0, tiled=True)
+
+    def to_image(rows):
+        return lax.all_to_all(rows, "seq", split_axis=0, concat_axis=1, tiled=True)
+
+    def from_image(rows):
+        return lax.all_to_all(
+            rows.reshape(1, length, -1), "seq", split_axis=1, concat_axis=0, tiled=True
+        )
+
+    tokens_low = to_image(tokens).reshape(length, model_width)
+    upstream = to_image(out_grad).reshape(length, model_width)
+    keep = to_image(filled).reshape(length) > 0
+    tokens_flat = tokens_low.astype(jnp.float32)
+    hidden_one = norm_apply(tokens_flat, gain_one, shift_one).astype(jnp.bfloat16)
+    qkv_bias = jnp.concatenate(
+        [b_qv[:model_width], jnp.zeros((model_width,), jnp.float32), b_qv[model_width:]]
+    )
+    projected = (jnp.dot(hidden_one, w_qkv, preferred_element_type=jnp.float32) + qkv_bias).astype(
+        jnp.bfloat16
+    )
+    heads_view = projected.reshape(length, 3, H, HD)
+    queries, keys_all, values_all = heads_view[:, 0], heads_view[:, 1], heads_view[:, 2]
+    attn_rows, logsum, top = attend_forward((queries, keys_all, values_all, keep))
+    head_max = lax.pmax(top, ("dp", "seq"))
+    middle = tokens_flat + (jnp.dot(attn_rows, w_out, preferred_element_type=jnp.float32) + b_out)
+    hidden_two = norm_apply(middle, gain_two, shift_two).astype(jnp.bfloat16)
+    pre_act = jnp.dot(hidden_two, w_up, preferred_element_type=jnp.float32) + b_up
+    activated = exact_gelu(pre_act).astype(jnp.bfloat16)
+    block_rows = middle + (jnp.dot(activated, w_down, preferred_element_type=jnp.float32) + b_down)
+    block_out = from_image(block_rows.astype(jnp.bfloat16)).reshape(tokens.shape)
+    upstream_f = upstream.astype(jnp.float32)
+    d_bias_down = jnp.sum(upstream_f, axis=0)
+    d_down = first_dot(activated, upstream)
+    act_grad = last_dot(upstream, w_down)
+    gelu_out, gelu_pull = jax.vjp(exact_gelu, pre_act)
+    pre_grad = gelu_pull(act_grad)[0].astype(jnp.bfloat16)
+    d_bias_up = column_sum(pre_grad)
+    d_up = first_dot(hidden_two, pre_grad)
+    hidden_two_grad = last_dot(pre_grad, w_up)
+    norm_out_two, pull_two = jax.vjp(norm_apply, middle, gain_two, shift_two)
+    mid_norm_grad, d_gain_two, d_shift_two = pull_two(hidden_two_grad)
+    middle_grad = upstream_f + mid_norm_grad
+    branch_grad = middle_grad.astype(jnp.bfloat16)
+    d_bias_out = column_sum(branch_grad)
+    d_out = first_dot(attn_rows, branch_grad)
+    attn_grad = last_dot(branch_grad, w_out).astype(jnp.bfloat16)
+    token_grads = attend_backward(
+        (queries, keys_all, values_all, keep, logsum, attn_grad.reshape(length, H, HD))
+    ).reshape(length, 3 * model_width)
+    d_qkv = first_dot(hidden_one, token_grads)
+    bias_sums = column_sum(token_grads)
+    d_bias_qv = jnp.concatenate([bias_sums[:model_width], bias_sums[2 * model_width :]])
+    first_grad = last_dot(token_grads, w_qkv)
+    norm_out_one, pull_one = jax.vjp(norm_apply, tokens_flat, gain_one, shift_one)
+    in_norm_grad, d_gain_one, d_shift_one = pull_one(first_grad)
+    tokens_grad = from_image((middle_grad + in_norm_grad).astype(jnp.bfloat16)).reshape(
+        tokens.shape
+    )
+
+    def reduce_matrix(term):
+        part = lax.psum_scatter(
+            term.astype(jnp.bfloat16), "dp", scatter_dimension=0, tiled=True
+        )
+        return lax.psum(part, "seq").astype(jnp.float32)
+
+    small_terms = [
+        d_gain_one,
+        d_shift_one,
+        d_bias_qv,
+        d_bias_out,
+        d_gain_two,
+        d_shift_two,
+        d_bias_up,
+        d_bias_down,
+    ]
+    shards = lax.axis_size("dp")
+    packed = jnp.concatenate([term.reshape(shards, -1) for term in small_terms], axis=1)
+    mine = lax.psum(
+        lax.psum_scatter(packed, "dp", scatter_dimension=0, tiled=True), "seq"
+    ).reshape(-1)
+    small_out, start = [], 0
+    for term in small_terms:
+        size = term.shape[0] // shards
+        small_out.append(mine[start : start + size])
+        start += size
+    s_gain_one, s_shift_one, s_qv, s_out, s_gain_two, s_shift_two, s_up, s_down = small_out
+    limit = clip_threshold.astype(jnp.float32)
+    root_factor = jnp.sqrt(limit / jnp.maximum(head_max, limit))
+    head_cols = jnp.repeat(root_factor, HD)
+    weight_scale = jnp.concatenate([head_cols, head_cols, jnp.ones((model_width,), jnp.float32)])
+    clipped_weight = (qkv_weight.astype(jnp.float32) * weight_scale[None, :]).astype(jnp.bfloat16)
+    bias_count = qv_bias.shape[0]
+    bias_scale = jnp.concatenate([head_cols, jnp.ones((model_width,), jnp.float32)])
+    shard_scale = lax.dynamic_slice_in_dim(
+        bias_scale, lax.axis_index("dp") * bias_count, bias_count
+    )
+    clipped_bias = (qv_bias.astype(jnp.float32) * shard_scale).astype(jnp.bfloat16)
+    return (
+        block_out,
+        tokens_grad,
+        s_gain_one,
+        s_shift_one,
+        reduce_matrix(d_qkv),
+        s_qv,
+        reduce_matrix(d_out),
+        s_out,
+        s_gain_two,
+        s_shift_two,
+        reduce_matrix(d_up),
+        s_up,
+        reduce_matrix(d_down),
+        s_down,
+        clipped_weight,
+        clipped_bias,
+        head_max,
+    )
+
+
+def local(*args):
+    if args[0].shape[0] == lax.axis_size("seq"):
+        return by_image_local(*args)
+    return by_head_local(*args)
+
+
 def solution(mesh):
     return jax.shard_map(
         local,

time: 811 us -> 730 us (0.900)
  blocking collectives: 237 us -> 110 us
  local copies, waits for them, and re-layouts: 104 us -> 45.3 us
  waiting for transfers between devices: 184 us -> 236 us
  other arithmetic: 61.1 us -> 92.5 us
  matrix products: 180 us -> 207 us
    all_gather x9 -> x1, blocking collectives: 162 us -> 9.17 us  [gather_small(): everyone = lax.all_gather(packed, 'dp', axis=0, tiled=False)]
    reduce_scatter x4, waiting for transfers between devices: 8.35 us -> 90.7 us  [reduce_matrix(): lax.psum_scatter(term.astype(jnp.bfloat16), 'dp', scatter_dimension=0, ti...]
    all_to_all x4, waiting for transfers between devices: 98.9 us -> 25 us  [the longest x2 18.1 us: to_image(): return lax.all_to_all(rows, 'seq', split_axis=0, concat_axis=1, tiled=True)]
    reshape x10 -> x4, local copies, waits for them, and re-layouts: 45.7 us -> 5.67 us  [the longest x2 5.59 us: from_image(): rows.reshape(1, length, -1)]
    all_gather x4, waiting for transfers between devices: 18.3 us -> 57.4 us  [the longest x1 44.8 us: by_image_local(): w_down = lax.all_gather(down_weight, 'dp', axis=0, tiled=True)]
    all_to_all x4 -> x1, local copies, waits for them, and re-layouts: 22.4 us -> 0.69 us  [to_image(): return lax.all_to_all(rows, 'seq', split_axis=0, concat_axis=1, tiled=True)]
    unnamed x0 -> x5, other arithmetic: none -> 20.2 us
    dynamic_update_slice x21 -> x0, local copies, waits for them, and re-layouts: 15.8 us -> none  [the longest x12 8.84 us: local(): lax.map(attend_forward, (queries, keys_all, values_all, keep_all))]
  transfers between devices with their start and end apart: 13 -> 13, of which waited for: 5 -> 7; matrix products, arithmetic and copies ran while one was open for 35% -> 38% of each run, Pallas kernels for 0% -> 0%
where the time goes in v1:
time: 730 us; the launch traced here: 722 us
  waiting for transfers between devices  236 us (32%)
  matrix products  207 us (28%)
  blocking collectives  110 us (15%)
  other arithmetic  92.5 us (13%)
  local copies, waits for them, and re-layouts  45.3 us (6%)
  starting transfers between devices  16.6 us (2%)
  between operations  15.6 us (2%)
    reduce_scatter x4, waiting for transfers between devices, reduce_matrix(): lax.psum_scatter(term.astype(jnp.bfloat16), 'dp', scatter_dimension=0, ti...  90.7 us
    psum x1, waiting for transfers between devices, reduce_matrix(): return lax.psum(part, 'seq').astype(jnp.float32)  59.8 us
    dot_general x4, matrix products, last_dot(): lax.dot_general(left_op, right_op, (((1,), (1,)), ((), ())), preferred_el...  53.8 us
    all_gather x1, waiting for transfers between devices, by_image_local(): w_down = lax.all_gather(down_weight, 'dp', axis=0, tiled=True)  44.8 us
    pmax x1, blocking collectives, by_image_local(): head_max = lax.pmax(top, ('dp', 'seq'))  39.9 us
    dot_general x4, matrix products, first_dot(): lax.dot_general(left_op, right_op, (((0,), (0,)), ((), ())), preferred_el...  31.6 us
    unnamed x104, local copies, waits for them, and re-layouts  28.4 us
    unnamed x1, blocking collectives  24.8 us
  transfers between devices with their start and end apart: 13, of which 7 were waited for; matrix products, arithmetic and copies ran while one was open for 38% of the time, Pallas kernels for 0%

profile of v1, /device:TPU:0, one launch (start us, length us, event | category | flops | bytes accessed | tf_op | source)
XLA Modules:
  0.0 722.3 jit_solution(2920349240570478617)
XLA Ops:
  10.8 11.7 %all_to_all.55 = s32[4,1,160]{2,1,0:T(1,128)S(1)} all-to-all(s32[4,1,160]{2,1,0:T(1,128)S(1)} %all_to_all.18), channel_id=1, replica_groups=mesh['dp'=8,'seq'=4] {'seq'}, dimensions={0} | all-to-all | bytes 5120 | tf_op jit(solution)/shard_map/all_to_all | solution.py:391
  22.4 3.5 all-to-all-start
  27.8 9.2 %all-gather.1 = bf16[8,1,1536]{2,1,0:T(2,128)(2,1)S(1)} all-gather(bf16[1,1,1536]{2,1,0:T(2,128)(2,1)S(1)} %reshape.393), channel_id=2, replica_groups=mesh['dp'=8,'seq'=4] {'dp'}, dimensions={0}, use_global_device_ids=true | all-gather | bytes 27648 | tf_op jit(solution)/shard_map/all_gather | solution.py:351
  38.0 18.1 %all-to-all-done = bf16[4,160,1024]{2,1,0:T(8,128)(2,1)S(1)} async-done(((bf16[4,160,1024]{2,1,0:T(8,128)(2,1)}), bf16[4,160,1024]{2,1,0:T(8,128)(2,1)S(1)}, u32[]{:S(2)}, u32[]{:S(2)}) %all-to-all-start) | async-done | bytes 1310752 | tf_op jit(solution)/shard_map/all_to_all | solution.py:391
  56.2 3.5 all-to-all-start.3
  60.7 1.6 fusion.25
  62.3 1.6 fusion.20
  63.9 9.4 %add_convert_fusion.1 = bf16[640,3072]{1,0:T(8,128)(2,1)} fusion(bf16[640,1024]{1,0:T(8,128)(2,1)} %fusion.20, bf16[1024,3072]{1,0:T(8,128)(2,1)} %all-gather.7.cloned.1.call-done, f32[3072]{0:T(1024)S(1)} %pad_maximum_fusion), kind=kOutput, calls=%fused_computation.32 | convolution fusion | flops 4030464000 | bytes 11546624 | tf_op jit(solution)/shard_map/dot_general | solution.py:406
  73.3 6.5 copy.56
  79.8 15.8 %fusion.48 = (f32[16,640]{1,0:T(8,128)S(1)}, f32[16,640,640]{1,2,0:T(8,128)}) fusion(pred[640]{0:T(1024)(128)(4,1)S(1)} %gt.23, bf16[640,3,16,64]{0,3,2,1:T(8,128)(2,1)} %bitcast.177), kind=kOutput, calls=%fused_computation.134 | convolution fusion | flops 858511360 | bytes 28877440 | tf_op jit(solution)/shard_map/qhd,khd->hqk/dot_general | solution.py:42
  95.6 15.3 %select_reduce_fusion = (f32[16]{0:T(128)}, f32[16,640]{1,0:T(8,128)S(1)}) fusion(f32[16,640,640]{1,2,0:T(8,128)} %get-tuple-element.58, pred[640,640]{0,1:T(8,128)(4,1)S(1)} %broadcast_and_fusion, f32[16,640]{1,0:T(8,128)S(1)} %get-tuple-element.57, pred[640]{0:T(1024)(128)(4,1)S(1)} %gt.23), kind=kLoop, calls=%fused_computation | loop fusion | flops 39311344 | bytes 26706624 | tf_op jit(solution)/shard_map/reduce_max | solution.py:61
  110.9 15.1 %fusion.31 = bf16[16,64,640]{2,1,0:T(8,128)(2,1)} fusion(f32[16,640]{1,0:T(8,128)S(1)} %get-tuple-element.18, f32[16,640]{1,0:T(8,128)S(1)} %get-tuple-element.57, bf16[640,3,16,64]{0,3,2,1:T(8,128)(2,1)} %bitcast.178, f32[16,640,640]{1,2,0:T(8,128)} %get-tuple-element.58, pred[640]{0:T(1024)(128)(4,1)S(1)} %gt.23), kind=kOutput, calls=%fused_computation.72 | convolution fusion | flops 872284160 | bytes 28918400 | tf_op jit(solution)/shard_map/hqk,khd->qhd/dot_general | solution.py:56
  126.0 3.9 fusion.54
  129.9 1.5 copy-done.5
  131.9 12.6 %all-gather.11.cloned.1.call-done = bf16[1024,4096]{1,0:T(8,128)(2,1)} async-done(((bf16[128,4096]{1,0:T(8,128)(2,1)}), bf16[1024,4096]{1,0:T(8,128)(2,1)}) %all-gather.11.cloned.1.call-update) | async-done | bytes 8388624 | tf_op jit(solution)/shard_map/all_gather | solution.py:387
  144.4 11.3 %fusion.47 = f32[640,4096]{1,0:T(8,128)} fusion(bf16[1024,4096]{1,0:T(8,128)(2,1)} %all-gather.11.cloned.1.call-done, f32[640,1024]{1,0:T(8,128)} %copy-done.5, f32[1024]{0:T(1024)S(1)} %get-tuple-element.42, f32[1024]{0:T(1024)S(1)} %get-tuple-element.43, f32[640]{0:T(1024)S(1)} %fusion.36, f32[640]{0:T(1024)S(1)} %broadcast_multiply_fusion), kind=kOutput, calls=%fused_computation.133 | convolution fusion | flops 5371985920 | bytes 21509120 | tf_op jit(solution)/shard_map/dot_general | solution.py:415
  155.8 44.8 %all-gather.13.cloned.1.call-done = bf16[4096,1024]{1,0:T(8,128)(2,1)} async-done(((bf16[512,1024]{1,0:T(8,128)(2,1)}), bf16[4096,1024]{1,0:T(8,128)(2,1)}) %all-gather.13.cloned.1.call-update) | async-done | bytes 8388624 | tf_op jit(solution)/shard_map/all_gather | solution.py:388
  200.6 33.4 %convert_reduce_fusion = (f32[4096]{0:T(1024)S(1)}, bf16[640,4096]{1,0:T(8,128)(2,1)S(1)}, f32[640,4096]{1,0:T(8,128)}) fusion(f32[640,4096]{1,0:T(8,128)} %fusion.47, f32[4096]{0:T(1024)S(1)} %bitcast.198, bf16[640,1024]{1,0:T(8,128)(2,1)S(1)} %bitcast.182, bf16[4096,1024]{1,0:T(8,128)(2,1)} %all-gather.13.cloned.1.call-done), kind=kOutput, calls=%fused_computation.14 | convolution fusion | flops 5565313024 | bytes 35946496 | tf_op jit(solution)/shard_map/dot_general | solution.py:26
  234.0 6.0 multiply_reduce_fusion.1
  240.1 0.8 fusion.52
  240.9 1.4 copy-done.3
  243.2 3.1 convolution_convert_fusion.3
  246.3 4.2 convolution_convert_fusion.4
  250.5 1.7 copy.59
  252.3 23.4 %multiply_reduce_fusion = (f32[16,640]{1,0:T(8,128)S(1)}, f32[16,640,640]{1,2,0:T(8,128)}) fusion(f32[16,640]{1,0:T(8,128)S(1)} %log_add_fusion, f32[16,640,640]{1,2,0:T(8,128)} %get-tuple-element.58, pred[640]{0:T(1024)(128)(4,1)S(1)} %gt.23, bf16[640,16,64]{0,2,1:T(8,128)(2,1)S(1)} %bitcast.188, bf16[640,3,16,64]{0,3,2,1:T(8,128)(2,1)} %bitcast.179), kind=kOutput, calls=%fused_computation.2 | convolution fusion | flops 871618560 | bytes 55132800 | tf_op jit(solution)/shard_map/qhd,khd->hqk/dot_general | solution.py:72
  275.6 23.2 %multiply_convert_fusion = bf16[16,640,640]{1,2,0:T(8,128)(2,1)} fusion(f32[16,640,640]{1,2,0:T(8,128)} %get-tuple-element.63, f32[16,640]{1,0:T(8,128)S(1)} %get-tuple-element.62, f32[16,640]{1,0:T(8,128)S(1)} %log_add_fusion, f32[16,640,640]{1,2,0:T(8,128)} %get-tuple-element.58, pred[640]{0:T(1024)(128)(4,1)S(1)} %gt.23), kind=kLoop, calls=%fused_computation.1 | loop fusion | flops 39321600 | bytes 65618560 | tf_op jit(solution)/shard_map/convert_element_type | solution.py:74
  298.8 10.1 %multiply_bitcast_fusion = bf16[640,1,16,64]{0,3,2,1:T(8,128)(2,1)} fusion(bf16[16,640,640]{1,2,0:T(8,128)(2,1)} %multiply_convert_fusion, bf16[640,3,16,64]{0,3,2,1:T(8,128)(2,1)S(1)} %bitcast.180), kind=kOutput, calls=%fused_computation.61 | convolution fusion | flops 840171520 | bytes 15728640 | tf_op jit(solution)/shard_map/hqk,qhd->khd/dot_general | solution.py:81
  308.9 8.0 %multiply_bitcast_fusion.1 = bf16[640,1,16,64]{0,3,2,1:T(8,128)(2,1)} fusion(bf16[16,640,640]{1,2,0:T(8,128)(2,1)} %multiply_convert_fusion, bf16[640,3,16,64]{0,3,2,1:T(8,128)(2,1)S(1)} %bitcast.181), kind=kOutput, calls=%fused_computation.62 | convolution fusion | flops 840171520 | bytes 15728640 | tf_op jit(solution)/shard_map/hqk,khd->qhd/dot_general | solution.py:77
  316.9 12.5 %fusion.27 = bf16[640,1,16,64]{0,3,2,1:T(8,128)(2,1)} fusion(bf16[640,16,64]{0,2,1:T(8,128)(2,1)S(1)} %bitcast.189, f32[16,640]{1,0:T(8,128)S(1)} %log_add_fusion, f32[16,640,640]{1,2,0:T(8,128)} %get-tuple-element.58, pred[640]{0:T(1024)(128)(4,1)S(1)} %gt.23), kind=kOutput, calls=%fused_computation.69 | convolution fusion | flops 865075200 | bytes 28877440 | tf_op jit(solution)/shard_map/hqk,qhd->khd/dot_general | solution.py:71
  329.4 2.5 convert_reduce_fusion.1
  332.0 2.0 copy-done.8
  333.9 7.5 %convolution_convert_fusion.2 = bf16[1024,3072]{1,0:T(8,128)(2,1)} fusion(bf16[640,1024]{1,0:T(8,128)(2,1)S(1)} %bitcast.192, bf16[640,3072]{0,1:T(8,128)(2,1)S(1)} %bitcast.190), kind=kOutput, calls=%fused_computation.35 | convolution fusion | flops 4029677568 | bytes 11534336 | tf_op jit(solution)/shard_map/dot_general | solution.py:32
  342.1 12.0 %convolution_convert_fusion = bf16[1024,4096]{1,0:T(8,128)(2,1)} fusion(bf16[640,4096]{1,0:T(8,128)(2,1)} %copy-done.37, f32[640,1024]{1,0:T(8,128)} %copy-done.5, f32[1024]{0:T(1024)S(1)} %copy-done.22, f32[1024]{0:T(1024)S(1)} %get-tuple-element.43, f32[640]{0:T(1024)S(1)} %fusion.36, f32[640]{0:T(1024)S(1)} %broadcast_multiply_fusion), kind=kOutput, calls=%fused_computation.33 | convolution fusion | flops 5376180224 | bytes 16266240 | tf_op jit(solution)/shard_map/dot_general | solution.py:32
  354.2 8.5 %multiply_convert_fusion.1 = bf16[640,4096]{1,0:T(8,128)(2,1)S(1)} fusion(f32[640,4096]{1,0:T(8,128)} %get-tuple-element.32, f32[640,4096]{1,0:T(8,128)} %fusion.47, f32[4096]{0:T(1024)S(1)} %bitcast.199), kind=kLoop, calls=%fused_computation.16 | loop fusion | flops 10485760 | bytes 26230784 | tf_op jit(solution)/shard_map/convert_element_type | solution.py:416
  362.7 2.4 copy-done.7
  365.1 9.0 %convolution_convert_fusion.1 = bf16[4096,1024]{1,0:T(8,128)(2,1)} fusion(bf16[640,4096]{1,0:T(8,128)(2,1)S(1)} %multiply_convert_fusion.1, bf16[640,1024]{1,0:T(8,128)(2,1)S(1)} %bitcast.183), kind=kOutput, calls=%fused_computation.34 | convolution fusion | flops 5372903424 | bytes 14942208 | tf_op jit(solution)/shard_map/dot_general | solution.py:32
  375.7 39.9 %pmax.7 = f32[16]{0:T(128)S(1)} all-reduce(f32[16]{0:T(128)S(1)} %copy-done.26), channel_id=1, replica_groups=mesh['dp'=8,'seq'=4] {'dp','seq'}, use_global_device_ids=true, to_apply=%region_30.31 | all-reduce | flops 16 | bytes 128 | tf_op jit(solution)/shard_map/pmax | solution.py:412
  416.4 1.0 multiply_convert_fusion.2
  417.4 11.8 %fusion.32 = bf16[1,640,1024]{2,1,0:T(8,128)(2,1)S(1)} fusion(f32[640,1024]{1,0:T(8,128)} %copy-done.5, bf16[640,4096]{1,0:T(8,128)(2,1)} %copy-done.7, bf16[4096,1024]{1,0:T(8,128)(2,1)} %all-gather.13.cloned.1.call-done, f32[1024]{0:T(1024)S(1)} %copy-done.20), kind=kOutput, calls=%fused_computation.74 | convolution fusion | flops 5370675200 | bytes 17567744 | tf_op jit(solution)/shard_map/dot_general | solution.py:417
  429.2 3.6 copy.79
  433.3 10.8 %reduce.12 = bf16[640,1024]{1,0:T(8,128)(2,1)} reduce(bf16[640,1,1024]{2,1,0:T(2,128)(2,1)} %bitcast.184, bf16[]{:T(256)} %broadcast.388), dimensions={1}, to_apply=%bitcast.176.reduce_sub_computation | reduce | bytes 2621442
  444.1 4.0 reshape.398
  448.0 4.3 all-to-all-start.2
  452.7 10.2 %fusion.49 = (f32[1024]{0:T(1024)S(1)}, f32[640]{0:T(1024)S(1)}, f32[640,1024]{1,0:T(8,128)}) fusion(f32[1024]{0:T(1024)S(1)} %copy-done.13, f32[640]{0:T(1024)S(1)} %copy-done.15, bf16[4,160,1024]{2,1,0:T(8,128)(2,1)S(1)} %copy-done.1, bf16[640,3072]{0,1:T(8,128)(2,1)} %bitcast.191, bf16[1024,3072]{1,0:T(8,128)(2,1)} %all-gather.7.cloned.1.call-done), kind=kOutput, calls=%fused_computation.135 | convolution fusion | flops 4030462464 | bytes 14169088 | tf_op jit(solution)/shard_map/dot_general | solution.py:26
  463.1 15.5 %reduce-scatter.9.cloned.1.call-done = bf16[128,4096]{1,0:T(8,128)(2,1)} async-done(((bf16[1024,4096]{1,0:T(8,128)(2,1)}), bf16[128,4096]{1,0:T(8,128)(2,1)}) %reduce-scatter.9.cloned.1.call-update) | async-done | bytes 1048592 | tf_op jit(solution)/shard_map/reduce_scatter | solution.py:449
  478.6 75.1 %reduce-scatter.11.cloned.1.call-done = bf16[512,1024]{1,0:T(8,128)(2,1)} async-done(((bf16[4096,1024]{1,0:T(8,128)(2,1)}), bf16[512,1024]{1,0:T(8,128)(2,1)}) %reduce-scatter.11.cloned.1.call-update) | async-done | bytes 1048592 | tf_op jit(solution)/shard_map/reduce_scatter | solution.py:449
  553.8 3.0 fusion.21
  556.9 2.7 fusion.33
  559.5 2.0 copy.78
  561.6 9.4 %reduce.13 = bf16[640,1024]{1,0:T(8,128)(2,1)} reduce(bf16[640,1,1024]{2,1,0:T(2,128)(2,1)S(1)} %bitcast.185, bf16[]{:T(256)} %broadcast.388), dimensions={1}, to_apply=%bitcast.175.reduce_sub_computation | reduce | bytes 2621442
  570.9 3.9 reshape.400
  574.9 4.6 all-to-all-start.4
  579.5 24.8 %all-reduce.1 = f32[8,1536]{1,0:T(8,128)S(1)} all-reduce(f32[8,1536]{1,0:T(8,128)S(1)} %constant_dynamic-update-slice_fusion), channel_id=3, replica_groups=mesh['dp'=8,'seq'=4] {'dp'}, use_global_device_ids=true, to_apply=%region_19.20.clone | all-reduce | flops 12288 | bytes 98304
  605.0 24.5 %psum.35 = f32[1,1536]{1,0:T(1,128)S(1)} all-reduce(f32[1,1536]{1,0:T(1,128)S(1)} %constant_dynamic-slice_fusion), channel_id=1, replica_groups=mesh['dp'=8,'seq'=4] {'seq'}, use_global_device_ids=true, to_apply=%region_20.21 | all-reduce | flops 1536 | bytes 12288 | tf_op jit(solution)/shard_map/psum | solution.py:466
  631.2 2.8 reshape.399
  634.1 1.5 copy.69
  635.6 6.8 all-to-all-done.4
  642.5 2.8 reshape.401
  645.3 1.5 copy.70
  646.9 59.8 %all-reduce.5.cloned.1.call-done = (bf16[128,3072]{1,0:T(8,128)(2,1)}, bf16[128,1024]{1,0:T(8,128)(2,1)}, bf16[128,4096]{1,0:T(8,128)(2,1)}, bf16[512,1024]{1,0:T(8,128)(2,1)}) async-done(((bf16[128,3072]{1,0:T(8,128)(2,1)}, bf16[128,1024]{1,0:T(8,128)(2,1)}, bf16[128,4096]{1,0:T(8,128)(2,1)}, bf16[512,1024]{1,0:T(8,128)(2,1)}), (bf16[128,3072]{1,0:T(8,128)(2,1)}, bf16[128,1024]{1,0:T(8,128)(2,1)}, ...) | async-done | bytes 3145744 | tf_op jit(solution)/shard_map/psum | solution.py:452
  706.7 1.9 convert_element_type.248
  708.6 2.4 convert_element_type.246
  711.0 2.8 convert_element_type.250
  713.8 1.6 convert_element_type.252
  (161 shorter events, 14.3 us)
Async XLA Ops:
  7.2 18.8 %copy-start.27 = (bf16[128]{0:T(256)(128)(2,1)S(1)}, bf16[128]{0:T(256)(128)(2,1)}, u32[]{:S(2)}) copy-start(bf16[128]{0:T(256)(128)(2,1)} %param.19) | copy-start | bytes 772
  7.2 19.1 %copy-start.28 = (bf16[128]{0:T(256)(128)(2,1)S(1)}, bf16[128]{0:T(256)(128)(2,1)}, u32[]{:S(2)}) copy-start(bf16[128]{0:T(256)(128)(2,1)} %param.20) | copy-start | bytes 772
  7.2 19.3 %copy-start.23 = (bf16[256]{0:T(256)(128)(2,1)S(1)}, bf16[256]{0:T(256)(128)(2,1)}, u32[]{:S(2)}) copy-start(bf16[256]{0:T(256)(128)(2,1)} %param.22) | copy-start | bytes 1540
  7.2 19.5 %copy-start.29 = (bf16[128]{0:T(256)(128)(2,1)S(1)}, bf16[128]{0:T(256)(128)(2,1)}, u32[]{:S(2)}) copy-start(bf16[128]{0:T(256)(128)(2,1)} %param.24) | copy-start | bytes 772
  7.2 19.7 %copy-start.30 = (bf16[128]{0:T(256)(128)(2,1)S(1)}, bf16[128]{0:T(256)(128)(2,1)}, u32[]{:S(2)}) copy-start(bf16[128]{0:T(256)(128)(2,1)} %param.25) | copy-start | bytes 772
  7.2 19.9 %copy-start.31 = (bf16[128]{0:T(256)(128)(2,1)S(1)}, bf16[128]{0:T(256)(128)(2,1)}, u32[]{:S(2)}) copy-start(bf16[128]{0:T(256)(128)(2,1)} %param.26) | copy-start | bytes 772
  7.3 20.1 %copy-start.25 = (bf16[512]{0:T(512)(128)(2,1)S(1)}, bf16[512]{0:T(512)(128)(2,1)}, u32[]{:S(2)}) copy-start(bf16[512]{0:T(512)(128)(2,1)} %param.28) | copy-start | bytes 3076
  7.3 20.3 %copy-start.32 = (bf16[128]{0:T(256)(128)(2,1)S(1)}, bf16[128]{0:T(256)(128)(2,1)}, u32[]{:S(2)}) copy-start(bf16[128]{0:T(256)(128)(2,1)} %param.30) | copy-start | bytes 772
  7.3 56.6 %all-gather.7.cloned.1.call-start = ((), (), s32[]{:S(2)}) async-start(), calls=%async_computation.9 | async-start | bytes 7077888 | tf_op jit(solution)/shard_map/all_gather | solution.py:379
  8.0 118.0 %all-gather.9.cloned.1.call-start = ((), (), s32[]{:S(2)}) async-start(), calls=%async_computation.10 | async-start | bytes 2359296 | tf_op jit(solution)/shard_map/all_gather | solution.py:386
  8.8 135.7 %all-gather.11.cloned.1.call-start = ((), (), s32[]{:S(2)}) async-start(), calls=%async_computation.11 | async-start | bytes 9437184 | tf_op jit(solution)/shard_map/all_gather | solution.py:387
  9.5 191.1 %all-gather.13.cloned.1.call-start = ((), (), s32[]{:S(2)}) async-start(), calls=%async_computation.12 | async-start | bytes 9437184 | tf_op jit(solution)/shard_map/all_gather | solution.py:388
  22.4 33.7 %all-to-all-start = ((bf16[4,160,1024]{2,1,0:T(8,128)(2,1)}), bf16[4,160,1024]{2,1,0:T(8,128)(2,1)S(1)}, u32[]{:S(2)}, u32[]{:S(2)}) async-start(bf16[4,160,1024]{2,1,0:T(8,128)(2,1)} %param.16), calls=%async_computation | async-start | bytes 2621440 | tf_op jit(solution)/shard_map/all_to_all | solution.py:391
  37.7 24.6 %copy-start.12 = (f32[1024]{0:T(1024)}, f32[1024]{0:T(1024)S(1)}, u32[]{:S(2)}) copy-start(f32[1024]{0:T(1024)S(1)} %get-tuple-element.46) | copy-start | bytes 12292
  37.7 106.8 %copy-start.21 = (f32[1024]{0:T(1024)}, f32[1024]{0:T(1024)S(1)}, u32[]{:S(2)}) copy-start(f32[1024]{0:T(1024)S(1)} %get-tuple-element.42) | copy-start | bytes 12292
  56.1 69.9 %copy-start = (bf16[4,160,1024]{2,1,0:T(8,128)(2,1)}, bf16[4,160,1024]{2,1,0:T(8,128)(2,1)S(1)}, u32[]{:S(2)}) copy-start(bf16[4,160,1024]{2,1,0:T(8,128)(2,1)S(1)} %all-to-all-done) | copy-start | bytes 3932164
  56.2 99.6 %all-to-all-start.3 = ((bf16[4,160,1024]{2,1,0:T(8,128)(2,1)}), bf16[4,160,1024]{2,1,0:T(8,128)(2,1)S(1)}, u32[]{:S(2)}, u32[]{:S(2)}) async-start(bf16[4,160,1024]{2,1,0:T(8,128)(2,1)} %param.18), calls=%async_computation.3 | async-start | bytes 2621440 | tf_op jit(solution)/shard_map/all_to_all | solution.py:391
  59.7 403.4 %reduce-scatter.7.cloned.1.call-start = ((), (), s32[]{:S(2)}) async-start(), calls=%async_computation.14 | async-start | bytes 2359296 | tf_op jit(solution)/shard_map/reduce_scatter | solution.py:449
  60.1 13.2 %copy-start.14 = (f32[640]{0:T(1024)}, f32[640]{0:T(1024)S(1)}, u32[]{:S(2)}) copy-start(f32[640]{0:T(1024)S(1)} %div.57) | copy-start | bytes 7684
  60.7 12.6 %copy-start.18 = (f32[640]{0:T(1024)}, f32[640]{0:T(1024)S(1)}, u32[]{:S(2)}) copy-start(f32[640]{0:T(1024)S(1)} %add.126) | copy-start | bytes 7684
  60.7 1.6 copy-start.16
  129.9 1.6 copy-start.5
  200.6 33.4 %copy-start.6 = (f32[640,1024]{1,0:T(8,128)S(1)}, f32[640,1024]{1,0:T(8,128)}, u32[]{:S(2)}) copy-start(f32[640,1024]{1,0:T(8,128)} %copy-done.5) | copy-start | bytes 7864324
  200.6 33.4 %copy-start.33 = (bf16[1024,4096]{1,0:T(8,128)(2,1)S(1)}, bf16[1024,4096]{1,0:T(8,128)(2,1)}, u32[]{:S(2)}) copy-start(bf16[1024,4096]{1,0:T(8,128)(2,1)} %all-gather.11.cloned.1.call-done) | copy-start | bytes 25165828
  234.0 6.1 copy-start.37
  240.9 1.5 copy-start.3
  240.9 2.3 copy-start.34
  252.2 210.9 %reduce-scatter.5.cloned.1.call-start = ((), (), s32[]{:S(2)}) async-start(), calls=%async_computation.13 | async-start | bytes 7077888 | tf_op jit(solution)/shard_map/reduce_scatter | solution.py:449
  275.6 23.2 %copy-start.2 = (bf16[640,3072]{0,1:T(8,128)(2,1)S(1)}, bf16[640,3072]{0,1:T(8,128)(2,1)}, u32[]{:S(2)}) copy-start(bf16[640,3072]{0,1:T(8,128)(2,1)} %copy.56) | copy-start | bytes 11796484
  329.4 4.5 copy-start.10
  332.0 2.0 copy-start.8
  341.4 0.7 copy-start.22
  341.5 137.2 %reduce-scatter.9.cloned.1.call-start = ((), (), s32[]{:S(2)}) async-start(), calls=%async_computation.15 | async-start | bytes 9437184 | tf_op jit(solution)/shard_map/reduce_scatter | solution.py:449
  354.1 199.6 %reduce-scatter.11.cloned.1.call-start = ((), (), s32[]{:S(2)}) async-start(), calls=%async_computation.16 | async-start | bytes 9437184 | tf_op jit(solution)/shard_map/reduce_scatter | solution.py:449
  362.7 2.4 copy-start.7
  374.1 0.8 copy-start.35
  374.1 1.6 copy-start.26
  374.1 41.7 %copy-start.24 = (bf16[256]{0:T(256)(128)(2,1)S(1)}, bf16[256]{0:T(256)(128)(2,1)}, u32[]{:S(2)}) copy-start(bf16[256]{0:T(256)(128)(2,1)} %param.22) | copy-start | bytes 1540
  374.1 42.3 %copy-start.9 = (bf16[128,3072]{1,0:T(8,128)(2,1)S(1)}, bf16[128,3072]{1,0:T(8,128)(2,1)}, u32[]{:S(2)}) copy-start(bf16[128,3072]{1,0:T(8,128)(2,1)} %param.21) | copy-start | bytes 2359300
  374.1 43.3 %copy-start.20 = (f32[1024]{0:T(1024)S(1)}, f32[1024]{0:T(1024)}, u32[]{:S(2)}) copy-start(f32[1024]{0:T(1024)} %get-tuple-element.41) | copy-start | bytes 12292
  415.6 13.6 %copy-start.36 = (f32[16]{0:T(128)}, f32[16]{0:T(128)S(1)}, u32[]{:S(2)}) copy-start(f32[16]{0:T(128)S(1)} %pmax.7) | copy-start | bytes 196
  433.3 19.4 %copy-start.1 = (bf16[4,160,1024]{2,1,0:T(8,128)(2,1)S(1)}, bf16[4,160,1024]{2,1,0:T(8,128)(2,1)}, u32[]{:S(2)}) copy-start(bf16[4,160,1024]{2,1,0:T(8,128)(2,1)} %copy-done) | copy-start | bytes 3932164
  433.3 19.4 %copy-start.13 = (f32[1024]{0:T(1024)S(1)}, f32[1024]{0:T(1024)}, u32[]{:S(2)}) copy-start(f32[1024]{0:T(1024)} %copy-done.12) | copy-start | bytes 12292
  433.3 19.4 %copy-start.15 = (f32[640]{0:T(1024)S(1)}, f32[640]{0:T(1024)}, u32[]{:S(2)}) copy-start(f32[640]{0:T(1024)} %copy-done.14) | copy-start | bytes 7684
  448.0 126.8 %all-to-all-start.2 = ((bf16[4,2,81920]{2,1,0:T(2,128)(2,1)}), bf16[4,2,81920]{2,1,0:T(2,128)(2,1)}, u32[]{:S(2)}, u32[]{:S(2)}) async-start(bf16[4,2,81920]{2,1,0:T(2,128)(2,1)} %reshape.398), calls=%async_computation.2 | async-start | bytes 2621440 | tf_op jit(solution)/shard_map/all_to_all | solution.py:394
  452.4 10.7 %copy-start.19 = (f32[640]{0:T(1024)S(1)}, f32[640]{0:T(1024)}, u32[]{:S(2)}) copy-start(f32[640]{0:T(1024)} %copy-done.18) | copy-start | bytes 7684
  452.4 101.4 %copy-start.17 = (f32[640]{0:T(1024)S(1)}, f32[640]{0:T(1024)}, u32[]{:S(2)}) copy-start(f32[640]{0:T(1024)} %copy-done.16) | copy-start | bytes 7684
  452.4 254.3 %all-reduce.5.cloned.1.call-start = ((), (), s32[]{:S(2)}) async-start(), calls=%async_computation.17 | async-start | bytes 6291456 | tf_op jit(solution)/shard_map/psum | solution.py:452
  553.8 3.1 copy-start.4
  574.9 67.6 %all-to-all-start.4 = ((bf16[4,2,81920]{2,1,0:T(2,128)(2,1)}), bf16[4,2,81920]{2,1,0:T(2,128)(2,1)}, u32[]{:S(2)}, u32[]{:S(2)}) async-start(bf16[4,2,81920]{2,1,0:T(2,128)(2,1)} %reshape.400), calls=%async_computation.4 | async-start | bytes 2621440 | tf_op jit(solution)/shard_map/all_to_all | solution.py:394
  706.7 7.1 copy-start.11
Sparse Core Ops, SparseCore 0:
  10.0 48.2 all-gather.6
  60.1 27.9 all-gather.8
  90.0 54.3 all-gather.10
  146.2 54.3 all-gather.12
  252.3 41.1 reduce-scatter.6
  341.6 62.0 reduce-scatter.4
  407.2 71.4 reduce-scatter.8
  482.5 71.2 reduce-scatter.10
  556.4 150.2 all-reduce.4

commit v2 on v1

--- a/solution.py
+++ b/solution.py
@@ -1,6 +1,10 @@
+import math
+
 import jax
 import jax.numpy as jnp
 from jax import lax
+from jax.experimental import pallas as pl
+from jax.experimental.pallas import tpu as pltpu
 from jax.sharding import PartitionSpec as P
 
 H = 16
@@ -345,15 +349,472 @@
     )
 
 
-def gather_small(pieces):
-    sizes = [piece.shape[0] for piece in pieces]
-    packed = jnp.concatenate(pieces)
-    everyone = lax.all_gather(packed, "dp", axis=0, tiled=False)
-    outs, start = [], 0
-    for size in sizes:
-        outs.append(everyone[:, start : start + size].reshape(-1))
-        start += size
-    return outs
+MESH = pl.DeviceIdType.MESH
+BF = jnp.bfloat16
+F32 = jnp.float32
+SMALL = (128, 128, 256, 128, 128, 128, 512, 128)
+
+
+def flip(d, m):
+    y = lax.rem(lax.div(d, 4) + m // 4, 2)
+    x = lax.rem(lax.rem(lax.div(d, 2), 2) + (m // 2) % 2, 2)
+    k = lax.rem(lax.rem(d, 2) + m % 2, 2)
+    return 4 * y + 2 * x + k
+
+
+def flip_traced(d, m):
+    y = lax.rem(lax.div(d, 4) + lax.div(m, 4), 2)
+    x = lax.rem(lax.rem(lax.div(d, 2), 2) + lax.rem(lax.div(m, 2), 2), 2)
+    k = lax.rem(lax.rem(d, 2) + lax.rem(m, 2), 2)
+    return 4 * y + 2 * x + k
+
+
+def dot_nn(a, b):
+    return lax.dot_general(a, b, (((1,), (0,)), ((), ())), preferred_element_type=F32)
+
+
+def dot_nt(a, b):
+    return lax.dot_general(a, b, (((1,), (1,)), ((), ())), preferred_element_type=F32)
+
+
+def dot_tn(a, b):
+    return lax.dot_general(a, b, (((0,), (0,)), ((), ())), preferred_element_type=F32)
+
+
+def rows_of(block, size, start=0, count=None):
+    count = size if count is None else count
+    step = math.gcd(size, start) if start else size
+    return pl.ds(pl.multiple_of(block * size + start, step), count)
+
+
+def normalized(v):
+    center = jnp.mean(v, axis=-1, keepdims=True)
+    centered = v - center
+    spread = jnp.mean(centered * centered, axis=-1, keepdims=True)
+    scale = lax.rsqrt(spread + epsilon)
+    return centered * scale, scale
+
+
+def half_masks():
+    lane = lax.broadcasted_iota(jnp.int32, (1, 2 * HD), 1)
+    low = jnp.where(lane < HD, 1.0, 0.0)
+    return low.astype(BF), (1.0 - low).astype(BF), lane < HD
+
+
+def front_kernel(
+    tok_in, grad_in, fil_in, wq_in, wo_in, wu_in, wd_in, small_in,
+    out_h, tok_h, h1_h, qkv_h, gx_h, go_h, dwo_h, dwu_h, dwd_h, wq_h,
+    vec_o, dbup_o, top_o, mask_o,
+    wq, wo, wu, wd, tok, grad, h1, qkv, att, x1, h2, h2t, y, dh, fil, small, col, dst, ust,
+    own_s, own_r, rel_s, rel_r, fwd_s, fwd_r, tok_s, tok_r, fil_s, fil_r, sm_s, sm_r, loc, stg, hout,
+):
+    d, s = lax.axis_index("dp"), lax.axis_index("seq")
+    images, part, width = tok_in.shape
+    length = images * part
+    pair_count = width // (2 * HD)
+    weights = ((wq_in, wq), (wo_in, wo), (wu_in, wu), (wd_in, wd))
+    sib, xn, yn, dn = flip(d, 1), flip(d, 2), flip(d, 4), flip(d, 6)
+
+    barrier = pltpu.get_barrier_semaphore()
+    for m in range(1, 8):
+        pl.semaphore_signal(barrier, inc=1, device_id=(flip(d, m), s), device_id_type=MESH)
+    for j in range(1, images):
+        pl.semaphore_signal(
+            barrier, inc=1, device_id=(d, lax.rem(s + j, images)), device_id_type=MESH
+        )
+    pl.semaphore_wait(barrier, 7 + images - 1)
+
+    def send(src, dst, ss, rs, to_dp, to_seq):
+        return pltpu.make_async_remote_copy(
+            src_ref=src, dst_ref=dst, send_sem=ss, recv_sem=rs,
+            device_id=(to_dp, to_seq), device_id_type=MESH,
+        )
+
+    def exchange(src, dst, ss, rs, rows):
+        copies = []
+        for j in range(1, images):
+            to = lax.rem(s + j, images)
+            copies.append(send(src.at[to], dst.at[rows], ss.at[j - 1], rs.at[j - 1], d, to))
+        return copies
+
+    my_rows = rows_of(s, part)
+    sm_copies = [
+        send(small_in, small.at[d], sm_s.at[m - 1], sm_r.at[m - 1], flip(d, m), s)
+        for m in range(1, 8)
+    ]
+    fil_copies = exchange(fil_in, fil, fil_s, fil_r, s)
+    tok_copies = exchange(tok_in, tok, tok_s.at[0], tok_r.at[0], my_rows)
+    grad_copies = exchange(grad_in, grad, tok_s.at[1], tok_r.at[1], my_rows)
+
+    def own(w):
+        src, dst = weights[w]
+        size = src.shape[0]
+        half = size // 2
+        def piece(way, to, h):
+            return send(
+                src.at[pl.ds(h * half, half)], dst.at[rows_of(d, size, h * half, half)],
+                own_s.at[w, way, h], own_r.at[w, way, h], to, s,
+            )
+        return [
+            piece(0, xn, 0), piece(1, yn, 1), piece(0, xn, 1), piece(1, yn, 0),
+            send(src, dst.at[rows_of(d, size)], own_s.at[w, 2, 0], own_r.at[w, 2, 0], sib, s),
+        ]
+
+    def relays(w):
+        dst = weights[w][1]
+        size = weights[w][0].shape[0]
+        half = size // 2
+        lower, upper = rows_of(xn, size, 0, half), rows_of(yn, size, half, half)
+        return [
+            send(dst.at[lower], dst.at[lower], rel_s.at[w, 0], rel_r.at[w, 0], yn, s),
+            send(dst.at[upper], dst.at[upper], rel_s.at[w, 1], rel_r.at[w, 1], xn, s),
+        ]
+
+    def forwards(w):
+        dst = weights[w][1]
+        size = weights[w][0].shape[0]
+        return [
+            send(dst.at[rows_of(b, size)], dst.at[rows_of(b, size)],
+                 fwd_s.at[w, i], fwd_r.at[w, i], sib, s)
+            for i, b in enumerate((xn, yn, dn))
+        ]
+
+    def start_own(w):
+        for copy in own(w):
+            copy.start()
+
+    def on_first(w):
+        mine, relay, forward = own(w), relays(w), forwards(w)
+        mine[0].wait_recv()
+        relay[0].start()
+        mine[1].wait_recv()
+        relay[1].start()
+        mine[2].wait_recv()
+        forward[0].start()
+        mine[3].wait_recv()
+        forward[1].start()
+
+    def on_diag(w):
+        relay = relays(w)
+        relay[0].wait_recv()
+        relay[1].wait_recv()
+        forwards(w)[2].start()
+
+    def on_sib(w):
+        own(w)[4].wait_recv()
+        for copy in forwards(w):
+            copy.wait_recv()
+
+    def drain(w):
+        for copy in own(w) + relays(w) + forwards(w):
+            copy.wait_send()
+
+    def keep_own(w):
+        src, dst = weights[w]
+        return pltpu.make_async_copy(src, dst.at[rows_of(d, src.shape[0])], loc.at[w])
+
+    for copy in sm_copies + fil_copies:
+        copy.start()
+    start_own(0)
+    for copy in tok_copies:
+        copy.start()
+    start_own(1)
+    locals_ = [keep_own(w) for w in range(4)]
+    locals_ += [
+        pltpu.make_async_copy(tok_in.at[s], tok.at[my_rows], loc.at[4]),
+        pltpu.make_async_copy(grad_in.at[s], grad.at[my_rows], loc.at[5]),
+        pltpu.make_async_copy(fil_in.at[s], fil.at[s], loc.at[6]),
+        pltpu.make_async_copy(small_in, small.at[d], loc.at[7]),
+    ]
+    for copy in locals_:
+        copy.start()
+
+    on_first(0)
+    start_own(2)
+
+    for copy in sm_copies + fil_copies:
+        copy.wait_recv()
+    for copy in locals_:
+        copy.wait()
+
+    starts = [sum(SMALL[:i]) for i in range(len(SMALL))]
+
+    def vector(i, first=0, last=8):
+        return jnp.concatenate(
+            [small[b, :, starts[i] : starts[i] + SMALL[i]] for b in range(first, last)], axis=1
+        )
+
+    mask = fil[0] + fil[1] + fil[2] + fil[3]
+    mask_o[...] = mask
+    col[...] = jnp.transpose(mask)
+
+    for copy in tok_copies:
+        copy.wait_recv()
+    for copy in grad_copies:
+        copy.start()
+
+    block = 128
+    gain1, shift1 = vector(0), vector(1)
+
+    @pl.loop(0, length // block)
+    def _(i):
+        r = rows_of(i, block)
+        xh, _ = normalized(tok[r, :].astype(F32))
+        h1[r, :] = (xh * gain1 + shift1).astype(BF)
+
+    on_diag(0)
+    on_first(1)
+    on_sib(0)
+
+    tile = 512
+    qkv_bias = jnp.concatenate(
+        [vector(2, 0, 4), jnp.zeros((1, width), F32), vector(2, 4, 8)], axis=1
+    )
+    y[pl.ds(0, 1), :] = qkv_bias[:, :width]
+    y[pl.ds(8, 1), :] = qkv_bias[:, width : 2 * width]
+    y[pl.ds(16, 1), :] = qkv_bias[:, 2 * width :]
+
+    for third in range(3):
+        @pl.loop(0, width // tile)
+        def _(n):
+            c = pl.ds(pl.multiple_of(n * tile, tile), tile)
+            cw = pl.ds(pl.multiple_of(third * width + n * tile, tile), tile)
+            value = dot_nn(h1[...], wq[:, cw]) + y[pl.ds(8 * third, 1), c]
+            qkv[:, cw] = value.astype(BF)
+
+    saves = [
+        pltpu.make_async_copy(tok, tok_h, hout.at[0]),
+        pltpu.make_async_copy(h1, h1_h, hout.at[1]),
+        pltpu.make_async_copy(qkv, qkv_h, hout.at[2]),
+        pltpu.make_async_copy(wq, wq_h, hout.at[3]),
+    ]
+    for copy in saves:
+        copy.start()
+
+    low, high, low_lane = half_masks()
+    pad = (mask[0:1, :] - 1.0) * 1e30
+    pad2 = jnp.concatenate([pad, pad], axis=1)
+    chunk = length // 2
+
+    def attend(p, carry):
+        c = pl.ds(pl.multiple_of(p * 2 * HD, 2 * HD), 2 * HD)
+        ck = pl.ds(pl.multiple_of(width + p * 2 * HD, 2 * HD), 2 * HD)
+        cv = pl.ds(pl.multiple_of(2 * width + p * 2 * HD, 2 * HD), 2 * HD)
+        k, v = qkv[:, ck], qkv[:, cv]
+        k2 = jnp.concatenate([k * low, k * high], axis=0)
+        v2 = jnp.concatenate([v * low, v * high], axis=0)
+        best = [jnp.full((1, 1), very_negative, F32)] * 2
+        for j in range(2):
+            r = pl.ds(j * chunk, chunk)
+            q = qkv[r, c] * jnp.asarray(HD ** (-0.5), BF)
+            scores = dot_nt(q, k2) + pad2
+            probs = []
+            for side in range(2):
+                part_s = scores[:, side * length : (side + 1) * length]
+                peak = jnp.max(part_s, axis=1, keepdims=True)
+                e = jnp.exp(part_s - peak)
+                total = jnp.sum(e, axis=1, keepdims=True)
+                probs.append((e * (1.0 / total)).astype(BF))
+                held = jnp.where(col[r, 0:1] > 0.5, peak, very_negative)
+                best[side] = jnp.maximum(best[side], jnp.max(held, axis=0, keepdims=True))
+            att[r, c] = dot_nn(jnp.concatenate(probs, axis=1), v2).astype(BF)
+        top_o[pl.ds(p, 1), :] = jnp.where(
+            low_lane, jnp.broadcast_to(best[0], (1, 2 * HD)), jnp.broadcast_to(best[1], (1, 2 * HD))
+        )
+        return carry
+
+    early = (pair_count * 5) // 8
+    lax.fori_loop(0, early, attend, 0)
+    on_first(2)
+    start_own(3)
+    lax.fori_loop(early, pair_count, attend, 0)
+    on_diag(1)
+    on_sib(1)
+
+    gain2, shift2, b_out, b_down = vector(4), vector(5), vector(3), vector(7)
+
+    @pl.loop(0, length // block)
+    def _(i):
+        r = rows_of(i, block)
+        mid = tok[r, :].astype(F32) + dot_nn(att[r, :], wo[...]) + b_out
+        x1[r, :] = mid
+        xh, _ = normalized(mid)
+        h2[r, :] = (xh * gain2 + shift2).astype(BF)
+
+    h2t[...] = jnp.transpose(h2[...])
+    dbup_o[...] = vector(6)
+    y[...] = x1[...] + b_down
+    dh[...] = jnp.zeros_like(dh)
+    for copy in grad_copies:
+        copy.wait_recv()
+
+    def add_grad(i, acc):
+        return acc + jnp.sum(grad[rows_of(i, block), :].astype(F32), axis=0, keepdims=True)
+
+    grad_sum = lax.fori_loop(0, length // block, add_grad, jnp.zeros((1, width), F32))
+
+    on_diag(2)
+    on_sib(2)
+
+    ff_block = wd_in.shape[0]
+
+    def stage_copies(slot, b):
+        cols = pl.ds(pl.multiple_of(b * ff_block, ff_block), ff_block)
+        return (
+            pltpu.make_async_copy(dst.at[slot], dwd_h.at[rows_of(b, ff_block)], stg.at[0, slot]),
+            pltpu.make_async_copy(ust.at[slot], dwu_h.at[:, cols], stg.at[1, slot]),
+        )
+
+    def mlp(i, carry):
+        b = flip_traced(d, i)
+        slot = lax.rem(i, 2)
+
+        @pl.when(i == 1)
+        def _():
+            own(3)[4].wait_recv()
+
+        @pl.when(i == 2)
+        def _():
+            on_first(3)
+
+        for at, which in ((3, 0), (5, 1), (7, 2)):
+            @pl.when(i == at)
+            def _():
+                forwards(3)[which].wait_recv()
+
+        @pl.when(i == 6)
+        def _():
+            on_diag(3)
+
+        cols = pl.ds(pl.multiple_of(b * ff_block, ff_block), ff_block)
+        rows = rows_of(b, ff_block)
+        u = dot_nn(h2[...], wu[:, cols]) + dbup_o[:, cols]
+        phi = 0.5 * (1.0 + lax.erf(u * (0.5**0.5)))
+        a = (u * phi).astype(BF)
+        slope = phi + u * (jnp.exp(-0.5 * u * u) * (1.0 / math.sqrt(2.0 * math.pi)))
+        gu_f = dot_nt(grad[...], wd[rows, :]) * slope
+        gu = gu_f.astype(BF)
+        y[...] += dot_nn(a, wd[rows, :])
+        dh[...] += dot_nt(gu, wu[:, cols])
+
+        @pl.when(i >= 2)
+        def _():
+            for copy in stage_copies(slot, b):
+                copy.wait()
+
+        dbup_o[:, cols] = jnp.sum(gu.astype(F32), axis=0, keepdims=True)
+        dst[slot] = dot_tn(a, grad[...]).astype(BF)
+        ust[slot] = dot_nn(h2t[...], gu).astype(BF)
+        for copy in stage_copies(slot, b):
+            copy.start()
+        return carry
+
+    lax.fori_loop(0, 8, mlp, 0)
+
+    for slot in range(2):
+        for copy in stage_copies(slot, d):
+            copy.wait()
+    for copy in saves:
+        copy.wait()
+    for w in range(4):
+        drain(w)
+    for copy in sm_copies + fil_copies + tok_copies + grad_copies:
+        copy.wait_send()
+
+    zero = jnp.zeros((1, width), F32)
+
+    def norm_back(i, acc):
+        r = rows_of(i, block)
+        h1[r, :] = y[r, :].astype(BF)
+        g = dh[r, :]
+        xh, scale = normalized(x1[r, :])
+        gg = g * gain2
+        inner = gg - jnp.mean(gg, axis=1, keepdims=True)
+        inner = inner - xh * jnp.mean(gg * xh, axis=1, keepdims=True)
+        total = grad[r, :].astype(F32) + scale * inner
+        dh[r, :] = total
+        low_total = total.astype(BF)
+        h2[r, :] = low_total
+        tok[r, :] = dot_nt(low_total, wo[...]).astype(BF)
+        return (
+            acc[0] + jnp.sum(g * xh, axis=0, keepdims=True),
+            acc[1] + jnp.sum(g, axis=0, keepdims=True),
+            acc[2] + jnp.sum(low_total.astype(F32), axis=0, keepdims=True),
+        )
+
+    sums = lax.fori_loop(0, length // block, norm_back, (zero, zero, zero))
+    finals = [
+        pltpu.make_async_copy(h1, out_h, hout.at[4]),
+        pltpu.make_async_copy(dh, gx_h, hout.at[5]),
+        pltpu.make_async_copy(tok, go_h, hout.at[6]),
+        pltpu.make_async_copy(wo, dwo_h, hout.at[7]),
+    ]
+    for copy in finals[:3]:
+        copy.start()
+    vec_o[pl.ds(0, 1), :] = sums[0]
+    vec_o[pl.ds(1, 1), :] = sums[1]
+    vec_o[pl.ds(2, 1), :] = sums[2]
+    vec_o[pl.ds(3, 1), :] = grad_sum
+    h2t[...] = jnp.transpose(att[...])
+
+    @pl.loop(0, width // tile)
+    def _(n):
+        c = pl.ds(pl.multiple_of(n * tile, tile), tile)
+        wo[:, c] = dot_nn(h2t[...], h2[:, c]).astype(BF)
+
+    finals[3].start()
+    for copy in finals:
+        copy.wait()
+
+
+def front(tokens, out_grad, filled_rows, qkv_weight, out_weight, up_weight, down_weight, small):
+    images, part, width = tokens.shape
+    length = images * part
+    shards = lax.axis_size("dp")
+    ff = up_weight.shape[1]
+    wide = qkv_weight.shape[1]
+    shape = jax.ShapeDtypeStruct
+    any_spec = pl.BlockSpec(memory_space=pl.ANY)
+    vmem_spec = pl.BlockSpec(memory_space=pltpu.VMEM)
+    dma = pltpu.SemaphoreType.DMA
+    vm = pltpu.VMEM
+    return pl.pallas_call(
+        front_kernel,
+        name="front",
+        out_shape=(
+            shape((length, width), BF),
+            shape((length, width), BF),
+            shape((length, width), BF),
+            shape((length, wide), BF),
+            shape((length, width), F32),
+            shape((length, width), BF),
+            shape((width, width), BF),
+            shape((width, ff), BF),
+            shape((ff, width), BF),
+            shape((width, wide), BF),
+            shape((8, width), F32),
+            shape((1, ff), F32),
+            shape((8, 2 * HD), F32),
+            shape((8, length), F32),
+        ),
+        in_specs=[any_spec] * 8,
+        out_specs=[any_spec] * 10 + [vmem_spec] * 4,
+        scratch_shapes=[
+            vm((width, wide), BF), vm((width, width), BF), vm((width, ff), BF), vm((ff, width), BF),
+            vm((length, width), BF), vm((length, width), BF), vm((length, width), BF),
+            vm((length, wide), BF), vm((length, width), BF), vm((length, width), F32),
+            vm((length, width), BF), vm((width, length), BF), vm((length, width), F32),
+            vm((length, width), F32), vm((images, 8, length), F32), vm((shards, 1, sum(SMALL)), F32),
+            vm((length, 8), F32), vm((2, down_weight.shape[0], width), BF),
+            vm((2, width, down_weight.shape[0]), BF),
+            dma((4, 3, 2)), dma((4, 3, 2)), dma((4, 2)), dma((4, 2)), dma((4, 3)), dma((4, 3)),
+            dma((2, images - 1)), dma((2, images - 1)), dma((images - 1,)), dma((images - 1,)),
+            dma((7,)), dma((7,)), dma((8,)), dma((2, 2)), dma((8,)),
+        ],
+        compiler_params=pltpu.CompilerParams(
+            collective_id=0, has_side_effects=True, vmem_limit_bytes=60 << 20
+        ),
+    )(tokens, out_grad, filled_rows, qkv_weight, out_weight, up_weight, down_weight, small)
 
 
 def by_image_local(
@@ -376,62 +837,37 @@
 ):
     images, local_rows, model_width = tokens.shape
     length = local_rows * images
-    w_qkv = lax.all_gather(qkv_weight, "dp", axis=0, tiled=True)
-    small = gather_small(
+    seq_index = lax.axis_index("seq")
+    small = jnp.concatenate(
         [norm1_gain, norm1_bias, qv_bias, out_bias, norm2_gain, norm2_bias, up_bias, down_bias]
-    )
-    gain_one, shift_one, b_qv, b_out, gain_two, shift_two, b_up, b_down = [
-        piece.astype(jnp.float32) for piece in small
-    ]
-    w_out = lax.all_gather(out_weight, "dp", axis=0, tiled=True)
-    w_up = lax.all_gather(up_weight, "dp", axis=0, tiled=True)
-    w_down = lax.all_gather(down_weight, "dp", axis=0, tiled=True)
-
-    def to_image(rows):
-        return lax.all_to_all(rows, "seq", split_axis=0, concat_axis=1, tiled=True)
+    ).astype(F32)[None]
+    flags = lax.dynamic_update_slice(
+        jnp.zeros((images, 8, length), F32),
+        jnp.broadcast_to((filled > 0).astype(F32)[:, None, :], (images, 8, local_rows)),
+        (0, 0, seq_index * local_rows),
+    )
+    (
+        block_rows, tokens_low, hidden_one, projected, middle_grad, attn_grad,
+        d_out, d_up, d_down, w_qkv, vec, d_bias_up, tops, mask,
+    ) = front(tokens, out_grad, flags, qkv_weight, out_weight, up_weight, down_weight, small)
+    gain_one = lax.all_gather(norm1_gain, "dp", axis=0, tiled=True).astype(F32)
+    shift_one = jnp.zeros_like(gain_one)
+    d_gain_two, d_shift_two, d_bias_out, d_bias_down = vec[0], vec[1], vec[2], vec[3]
+    d_bias_up = d_bias_up[0]
+    keep = mask[0] > 0.5
+    head_max = lax.pmax(tops[:, ::HD].reshape(-1), ("dp", "seq"))
+    tokens_flat = tokens_low.astype(F32)
 
     def from_image(rows):
         return lax.all_to_all(
             rows.reshape(1, length, -1), "seq", split_axis=1, concat_axis=0, tiled=True
         )
 
-    tokens_low = to_image(tokens).reshape(length, model_width)
-    upstream = to_image(out_grad).reshape(length, model_width)
-    keep = to_image(filled).reshape(length) > 0
-    tokens_flat = tokens_low.astype(jnp.float32)
-    hidden_one = norm_apply(tokens_flat, gain_one, shift_one).astype(jnp.bfloat16)
-    qkv_bias = jnp.concatenate(
-        [b_qv[:model_width], jnp.zeros((model_width,), jnp.float32), b_qv[model_width:]]
-    )
-    projected = (jnp.dot(hidden_one, w_qkv, preferred_element_type=jnp.float32) + qkv_bias).astype(
-        jnp.bfloat16
-    )
+    block_out = from_image(block_rows).reshape(tokens.shape)
     heads_view = projected.reshape(length, 3, H, HD)
     queries, keys_all, values_all = heads_view[:, 0], heads_view[:, 1], heads_view[:, 2]
-    attn_rows, logsum, top = attend_forward((queries, keys_all, values_all, keep))
-    head_max = lax.pmax(top, ("dp", "seq"))
-    middle = tokens_flat + (jnp.dot(attn_rows, w_out, preferred_element_type=jnp.float32) + b_out)
-    hidden_two = norm_apply(middle, gain_two, shift_two).astype(jnp.bfloat16)
-    pre_act = jnp.dot(hidden_two, w_up, preferred_element_type=jnp.float32) + b_up
-    activated = exact_gelu(pre_act).astype(jnp.bfloat16)
-    block_rows = middle + (jnp.dot(activated, w_down, preferred_element_type=jnp.float32) + b_down)
-    block_out = from_image(block_rows.astype(jnp.bfloat16)).reshape(tokens.shape)
-    upstream_f = upstream.astype(jnp.float32)
-    d_bias_down = jnp.sum(upstream_f, axis=0)
-    d_down = first_dot(activated, upstream)
-    act_grad = last_dot(upstream, w_down)
-    gelu_out, gelu_pull = jax.vjp(exact_gelu, pre_act)
-    pre_grad = gelu_pull(act_grad)[0].astype(jnp.bfloat16)
-    d_bias_up = column_sum(pre_grad)
-    d_up = first_dot(hidden_two, pre_grad)
-    hidden_two_grad = last_dot(pre_grad, w_up)
-    norm_out_two, pull_two = jax.vjp(norm_apply, middle, gain_two, shift_two)
-    mid_norm_grad, d_gain_two, d_shift_two = pull_two(hidden_two_grad)
-    middle_grad = upstream_f + mid_norm_grad
-    branch_grad = middle_grad.astype(jnp.bfloat16)
-    d_bias_out = column_sum(branch_grad)
-    d_out = first_dot(attn_rows, branch_grad)
-    attn_grad = last_dot(branch_grad, w_out).astype(jnp.bfloat16)
+    masked = score_block(queries, keys_all, keep)[1]
+    logsum = jax.nn.logsumexp(masked, axis=-1, keepdims=True)
     token_grads = attend_backward(
         (queries, keys_all, values_all, keep, logsum, attn_grad.reshape(length, H, HD))
     ).reshape(length, 3 * model_width)
@@ -505,7 +941,7 @@
 
 
 def local(*args):
-    if args[0].shape[0] == lax.axis_size("seq"):
+    if args[0].shape[0] == lax.axis_size("seq") and lax.axis_size("dp") == 8:
         return by_image_local(*args)
     return by_head_local(*args)
 

time: 730 us -> 665 us (0.911)
  Pallas kernels: 0 us -> 141 us
  matrix products: 207 us -> 84.2 us
  waiting for transfers between devices: 236 us -> 189 us
  other arithmetic: 92.5 us -> 71.4 us
  blocking collectives: 110 us -> 101 us
  starting transfers between devices: 16.6 us -> 8.96 us
    pallas_call x0 -> x1, Pallas kernels: none -> 141 us  [front(): pl.pallas_call(front_kernel, name='front', out_shape=(shape((length, widt...]
    reduce_scatter x4, waiting for transfers between devices: 90.7 us -> 165 us  [reduce_matrix(): lax.psum_scatter(term.astype(jnp.bfloat16), 'dp', scatter_dimension=0, ti...]
    all_gather x4 -> x0, waiting for transfers between devices: 57.4 us -> none  [the longest x1 44.8 us: by_image_local(): w_down = lax.all_gather(down_weight, 'dp', axis=0, tiled=True)]
    dot_general x5 -> x0, matrix products: 51.5 us -> none  [the longest x1 15.1 us: attend_forward(): jnp.einsum('hqk,khd->qhd', soft_probs, values_in, preferred_element_type=...]
    psum x1, waiting for transfers between devices: 59.8 us -> 11.9 us  [reduce_matrix(): return lax.psum(part, 'seq').astype(jnp.float32)]
    dot_general x4 -> x1, matrix products: 53.8 us -> 8.48 us  [last_dot(): lax.dot_general(left_op, right_op, (((1,), (1,)), ((), ())), preferred_el...]
    dot_general x4 -> x1, matrix products: 31.6 us -> 7.03 us  [first_dot(): lax.dot_general(left_op, right_op, (((0,), (0,)), ((), ())), preferred_el...]
    all_to_all x2 -> x0, waiting for transfers between devices: 18.1 us -> none  [to_image(): return lax.all_to_all(rows, 'seq', split_axis=0, concat_axis=1, tiled=True)]
  transfers between devices with their start and end apart: 13 -> 7, of which waited for: 7 -> 5; matrix products, arithmetic and copies ran while one was open for 38% -> 28% of each run, Pallas kernels for 0% -> 0%
where the time goes in v2:
time: 665 us; the launch traced here: 655 us
  waiting for transfers between devices  189 us (28%)
  Pallas kernels  141 us (21%)
  blocking collectives  101 us (15%)
  matrix products  84.2 us (13%)
  other arithmetic  71.4 us (11%)
  local copies, waits for them, and re-layouts  44.1 us (7%)
  between operations  15.2 us (2%)
  starting transfers between devices  8.96 us (1%)
    reduce_scatter x4, waiting for transfers between devices, reduce_matrix(): lax.psum_scatter(term.astype(jnp.bfloat16), 'dp', scatter_dimension=0, ti...  165 us
    pallas_call x1, Pallas kernels, front(): pl.pallas_call(front_kernel, name='front', out_shape=(shape((length, widt...  141 us
    pmax x1, blocking collectives, by_image_local(): head_max = lax.pmax(tops[:, ::HD].reshape(-1), ('dp', 'seq'))  44.3 us
    unnamed x56, local copies, waits for them, and re-layouts  26.8 us
    unnamed x1, blocking collectives  24.7 us
    convert_element_type x1, other arithmetic, attend_backward(): score_grad = (soft_probs * (prob_grad - inner_sum)).astype(jnp.bfloat16)  23.2 us
    dot_general x1, matrix products, attend_backward(): jnp.einsum('qhd,khd->hqk', upstream, values_in, preferred_element_type=jn...  22.9 us
    psum x1, blocking collectives, by_image_local(): lax.psum(lax.psum_scatter(packed, 'dp', scatter_dimension=0, tiled=True),...  22.7 us
  transfers between devices with their start and end apart: 7, of which 5 were waited for; matrix products, arithmetic and copies ran while one was open for 28% of the time, Pallas kernels for 0%

profile of v2, /device:TPU:0, one launch (start us, length us, event | category | flops | bytes accessed | tf_op | source)
XLA Modules:
  0.0 654.8 jit_solution(10986634807026036444)
XLA Ops:
  7.2 0.7 compare_convert_fusion
  7.9 0.7 constant_dynamic-update-slice_fusion.7
  8.6 0.7 constant_dynamic-update-slice_fusion.6
  9.3 0.7 constant_dynamic-update-slice_fusion.5
  9.9 0.7 constant_dynamic-update-slice_fusion.4
  10.6 0.7 constant_dynamic-update-slice_fusion.3
  11.2 0.7 constant_dynamic-update-slice_fusion.2
  11.9 0.7 constant_dynamic-update-slice_fusion.1
  12.6 0.7 constant_dynamic-update-slice_fusion
  13.3 0.6 convert_element_type.71.small_in
  14.2 0.6 copy-done.8
  14.8 141.0 %front.1 = (bf16[640,1024]{1,0:T(8,128)(2,1)}, bf16[640,1024]{1,0:T(8,128)(2,1)}, bf16[640,1024]{1,0:T(8,128)(2,1)}, bf16[640,3072]{1,0:T(8,128)(2,1)}, f32[640,...) custom-call(bf16[4,160,1024]{2,1,0:T(8,128)(2,1)} %tok_in.1, ...), custom_call_target="tpu_custom_call" | custom-call | tf_op jit(solution)/shard_map/front/pallas_call | solution.py:781
  155.9 0.8 compare_reduce_fusion
  157.2 0.7 copy.55
  157.9 6.4 copy.54
  164.2 16.2 %fusion = (f32[16,640]{1,0:T(8,128)S(1)}, f32[16,640,640]{1,2,0:T(8,128)}) fusion(pred[640]{0:T(1024)(128)(4,1)S(1)} %compare_reduce_fusion, bf16[640,3,16,64]{0,3,2,1:T(8,128)(2,1)} %bitcast.90), kind=kOutput, calls=%fused_computation.5 | convolution fusion | flops 858511360 | bytes 28877440 | tf_op jit(solution)/shard_map/qhd,khd->hqk/dot_general | solution.py:46
  180.5 12.0 %exponential_reduce_fusion = f32[16,640]{1,0:T(8,128)S(1)} fusion(f32[16,640,640]{1,2,0:T(8,128)} %get-tuple-element.71, f32[16,640]{1,0:T(8,128)S(1)} %is-finite_select_fusion, pred[640]{0:T(1024)(128)(4,1)S(1)} %compare_reduce_fusion), kind=kLoop, calls=%fused_computation.3 | loop fusion | flops 26204160 | bytes 26296960 | tf_op jit(solution)/shard_map/reduce_sum | solution.py:870
  192.5 22.9 %multiply_reduce_fusion = (f32[16,640]{1,0:T(8,128)S(1)}, f32[16,640,640]{1,2,0:T(8,128)}) fusion(f32[16,640,640]{1,2,0:T(8,128)} %get-tuple-element.71, f32[16,640]{1,0:T(8,128)S(1)} %log_add_fusion, pred[640]{0:T(1024)(128)(4,1)S(1)} %compare_reduce_fusion, bf16[640,16,64]{0,2,1:T(8,128)(2,1)S(1)} %bitcast.98, bf16[640,3,16,64]{0,3,2,1:T(8,128)(2,1)} %bitcast.91), kind=kOutput, calls=%fused_computation.1 | convolution fusion | flops 871618560 | bytes 55132800 | tf_op jit(solution)/shard_map/qhd,khd->hqk/dot_general | solution.py:76
  215.4 23.2 %multiply_convert_fusion = bf16[16,640,640]{1,2,0:T(8,128)(2,1)} fusion(f32[16,640,640]{1,2,0:T(8,128)} %get-tuple-element.73, f32[16,640,640]{1,2,0:T(8,128)} %get-tuple-element.71, f32[16,640]{1,0:T(8,128)S(1)} %get-tuple-element.72, f32[16,640]{1,0:T(8,128)S(1)} %log_add_fusion, pred[640]{0:T(1024)(128)(4,1)S(1)} %compare_reduce_fusion), kind=kLoop, calls=%fused_computation | loop fusion | flops 39321600 | bytes 65618560 | tf_op jit(solution)/shard_map/convert_element_type | solution.py:78
  238.6 10.1 %multiply_bitcast_fusion = bf16[640,1,16,64]{0,3,2,1:T(8,128)(2,1)} fusion(bf16[16,640,640]{1,2,0:T(8,128)(2,1)} %multiply_convert_fusion, bf16[640,3,16,64]{0,3,2,1:T(8,128)(2,1)S(1)} %bitcast.92), kind=kOutput, calls=%fused_computation.24 | convolution fusion | flops 840171520 | bytes 15728640 | tf_op jit(solution)/shard_map/hqk,qhd->khd/dot_general | solution.py:85
  248.7 7.0 %multiply_bitcast_fusion.1 = bf16[640,1,16,64]{0,3,2,1:T(8,128)(2,1)S(1)} fusion(bf16[16,640,640]{1,2,0:T(8,128)(2,1)} %multiply_convert_fusion, bf16[640,3,16,64]{0,3,2,1:T(8,128)(2,1)S(1)} %bitcast.93), kind=kOutput, calls=%fused_computation.25 | convolution fusion | flops 840171520 | bytes 15728640 | tf_op jit(solution)/shard_map/hqk,khd->qhd/dot_general | solution.py:81
  255.7 12.5 %fusion.13 = bf16[640,1,16,64]{0,3,2,1:T(8,128)(2,1)} fusion(bf16[640,16,64]{0,2,1:T(8,128)(2,1)S(1)} %bitcast.99, f32[16,640,640]{1,2,0:T(8,128)} %get-tuple-element.71, f32[16,640]{1,0:T(8,128)S(1)} %log_add_fusion, pred[640]{0:T(1024)(128)(4,1)S(1)} %compare_reduce_fusion), kind=kOutput, calls=%fused_computation.26 | convolution fusion | flops 865075200 | bytes 28877440 | tf_op jit(solution)/shard_map/hqk,qhd->khd/dot_general | solution.py:75
  268.2 2.2 convert_reduce_fusion
  270.3 1.9 copy-done.2
  272.3 7.0 %convolution_convert_fusion = bf16[1024,3072]{1,0:T(8,128)(2,1)} fusion(bf16[640,1024]{1,0:T(8,128)(2,1)S(1)} %copy-done.14, bf16[640,3072]{0,1:T(8,128)(2,1)S(1)} %bitcast.100), kind=kOutput, calls=%fused_computation.11 | convolution fusion | flops 4029677568 | bytes 11534336 | tf_op jit(solution)/shard_map/dot_general | solution.py:36
  279.4 0.7 reduce-scatter.9.cloned.1.call-update
  280.6 3.3 copy.68
  284.0 0.5 broadcast.92
  284.5 9.4 %reduce.7 = bf16[640,1024]{1,0:T(8,128)(2,1)} reduce(bf16[640,1,1024]{2,1,0:T(2,128)(2,1)S(1)} %bitcast.94, bf16[]{:T(256)} %broadcast.92), dimensions={1}, to_apply=%bitcast.89.reduce_sub_computation | reduce | bytes 2621442
  293.9 4.0 reshape.273
  297.9 4.3 all-to-all-start
  302.3 8.9 %all-gather = bf16[8,1,128]{2,1,0:T(2,128)(2,1)S(1)} all-gather(bf16[1,1,128]{2,1,0:T(2,128)(2,1)S(1)} %bitcast.114), channel_id=1, replica_groups=mesh['dp'=8,'seq'=4] {'dp'}, dimensions={0}, use_global_device_ids=true | all-gather | bytes 2304 | tf_op jit(solution)/shard_map/all_gather | solution.py:853
  311.5 8.5 %fusion.25 = (f32[1024]{0:T(1024)S(1)}, f32[640]{0:T(1024)S(1)}, f32[640]{0:T(1024)S(1)}, f32[640,1024]{1,0:T(8,128)S(1)}) fusion(f32[1024]{0:T(1024)S(1)} %bitcast.105, f32[640]{0:T(1024)S(1)} %broadcast_multiply_fusion, bf16[640,1024]{1,0:T(8,128)(2,1)S(1)} %copy-done.1, bf16[640,3072]{0,1:T(8,128)(2,1)} %bitcast.101, ...), kind=kOutput, calls=%fused_computation.74 | convolution fusion | flops 4031772672 | bytes 14171648 | tf_op jit(solution)/shard_map/dot_general | solution.py:30
  320.1 1.2 fusion.12
  321.2 0.5 copy-done.4
  321.8 1.9 fusion.16
  323.7 15.6 %reduce-scatter.5.cloned.1.call-done = bf16[128,3072]{1,0:T(8,128)(2,1)} async-done(((bf16[1024,3072]{1,0:T(8,128)(2,1)}), bf16[128,3072]{1,0:T(8,128)(2,1)}) %reduce-scatter.5.cloned.1.call-update) | async-done | bytes 786448 | tf_op jit(solution)/shard_map/reduce_scatter | solution.py:885
  339.3 74.8 %reduce-scatter.9.cloned.1.call-done = bf16[128,4096]{1,0:T(8,128)(2,1)} async-done(((bf16[1024,4096]{1,0:T(8,128)(2,1)}), bf16[128,4096]{1,0:T(8,128)(2,1)}) %reduce-scatter.9.cloned.1.call-update) | async-done | bytes 1048592 | tf_op jit(solution)/shard_map/reduce_scatter | solution.py:885
  414.1 75.0 %reduce-scatter.11.cloned.1.call-done = bf16[512,1024]{1,0:T(8,128)(2,1)} async-done(((bf16[4096,1024]{1,0:T(8,128)(2,1)}), bf16[512,1024]{1,0:T(8,128)(2,1)}) %reduce-scatter.11.cloned.1.call-update) | async-done | bytes 1048592 | tf_op jit(solution)/shard_map/reduce_scatter | solution.py:885
  489.1 44.3 %pmax.7 = f32[16]{0:T(128)S(1)} all-reduce(f32[16]{0:T(128)S(1)} %reshape.257), channel_id=1, replica_groups=mesh['dp'=8,'seq'=4] {'dp','seq'}, use_global_device_ids=true, to_apply=%region_20.21 | all-reduce | flops 16 | bytes 128 | tf_op jit(solution)/shard_map/pmax | solution.py:858
  534.0 0.7 reduce.6
  534.8 3.3 copy.67
  538.2 9.4 %reduce.8 = bf16[640,1024]{1,0:T(8,128)(2,1)} reduce(bf16[640,1,1024]{2,1,0:T(2,128)(2,1)S(1)} %bitcast.95, bf16[]{:T(256)} %broadcast.92), dimensions={1}, to_apply=%bitcast.88.reduce_sub_computation | reduce | bytes 2621442
  547.6 4.0 reshape.275
  551.6 0.6 dynamic-slice
  552.2 4.3 all-to-all-start.1
  556.6 24.7 %all-reduce.1 = f32[8,1536]{1,0:T(8,128)S(1)} all-reduce(f32[8,1536]{1,0:T(8,128)S(1)} %constant_dynamic-update-slice_fusion.8), channel_id=2, replica_groups=mesh['dp'=8,'seq'=4] {'dp'}, use_global_device_ids=true, to_apply=%region_10.11.clone | all-reduce | flops 12288 | bytes 98304
  581.3 0.7 constant_dynamic-slice_fusion
  582.0 22.7 %psum.35 = f32[1,1536]{1,0:T(1,128)S(1)} all-reduce(f32[1,1536]{1,0:T(1,128)S(1)} %constant_dynamic-slice_fusion), channel_id=1, replica_groups=mesh['dp'=8,'seq'=4] {'seq'}, use_global_device_ids=true, to_apply=%region_11.12 | all-reduce | flops 1536 | bytes 12288 | tf_op jit(solution)/shard_map/psum | solution.py:902
  604.7 0.6 slice.125
  605.3 0.6 slice.129
  606.7 0.6 fusion.21
  607.3 0.5 slice_bitcast_fusion.8
  607.8 1.0 multiply_convert_fusion.1
  608.8 2.8 reshape.274
  611.7 1.5 copy.63
  613.2 10.9 %all-to-all-done.1 = bf16[4,2,81920]{2,1,0:T(2,128)(2,1)} async-done(((bf16[4,2,81920]{2,1,0:T(2,128)(2,1)}), bf16[4,2,81920]{2,1,0:T(2,128)(2,1)}, u32[]{:S(2)}, u32[]{:S(2)}) %all-to-all-start.1) | async-done | bytes 1310752 | tf_op jit(solution)/shard_map/all_to_all | solution.py:862
  624.1 2.9 reshape.276
  626.9 1.5 copy.64
  628.5 11.9 %all-reduce.5.cloned.1.call-done = (bf16[128,3072]{1,0:T(8,128)(2,1)}, bf16[128,1024]{1,0:T(8,128)(2,1)}, bf16[128,4096]{1,0:T(8,128)(2,1)}, bf16[512,1024]{1,0:T(8,128)(2,1)}) async-done(((bf16[128,3072]{1,0:T(8,128)(2,1)}, bf16[128,1024]{1,0:T(8,128)(2,1)}, bf16[128,4096]{1,0:T(8,128)(2,1)}, bf16[512,1024]{1,0:T(8,128)(2,1)}), (bf16[128,3072]{1,0:T(8,128)(2,1)}, bf16[128,1024]{1,0:T(8,128)(2,1)}, ...) | async-done | bytes 3145744 | tf_op jit(solution)/shard_map/psum | solution.py:888
  640.3 1.9 convert_element_type.82
  642.2 2.5 convert_element_type.81
  644.7 1.5 convert_element_type.83
  646.3 1.6 convert_element_type.84
  (73 shorter events, 2.9 us)
Async XLA Ops:
  7.2 316.5 %reduce-scatter.7.cloned.1.call-start = ((), (), s32[]{:S(2)}) async-start(), calls=%async_computation.7 | async-start | bytes 2359296 | tf_op jit(solution)/shard_map/reduce_scatter | solution.py:885
  14.2 0.6 copy-start.8
  155.8 1.3 copy-start.5
  155.9 183.4 %reduce-scatter.5.cloned.1.call-start = ((), (), s32[]{:S(2)}) async-start(), calls=%async_computation.6 | async-start | bytes 7077888 | tf_op jit(solution)/shard_map/reduce_scatter | solution.py:885
  215.4 23.3 %copy-start = (bf16[640,3072]{0,1:T(8,128)(2,1)S(1)}, bf16[640,3072]{0,1:T(8,128)(2,1)}, u32[]{:S(2)}) copy-start(bf16[640,3072]{0,1:T(8,128)(2,1)} %copy.54) | copy-start | bytes 11796484
  268.2 4.1 copy-start.14
  270.3 1.9 copy-start.2
  279.3 134.7 %reduce-scatter.9.cloned.1.call-start = ((), (), s32[]{:S(2)}) async-start(), calls=%async_computation.8 | async-start | bytes 9437184 | tf_op jit(solution)/shard_map/reduce_scatter | solution.py:885
  280.1 209.0 %reduce-scatter.11.cloned.1.call-start = ((), (), s32[]{:S(2)}) async-start(), calls=%async_computation.9 | async-start | bytes 9437184 | tf_op jit(solution)/shard_map/reduce_scatter | solution.py:885
  293.9 8.4 %copy-start.12 = (bf16[128]{0:T(256)(128)(2,1)S(1)}, bf16[128]{0:T(256)(128)(2,1)}, u32[]{:S(2)}) copy-start(bf16[128]{0:T(256)(128)(2,1)} %param.19) | copy-start | bytes 772
  293.9 17.3 %copy-start.11 = (f32[8,128]{1,0:T(8,128)S(1)}, f32[8,128]{1,0:T(8,128)}, u32[]{:S(2)}) copy-start(f32[8,128]{1,0:T(8,128)} %get-tuple-element.44) | copy-start | bytes 12292
  293.9 17.4 %copy-start.1 = (bf16[640,1024]{1,0:T(8,128)(2,1)S(1)}, bf16[640,1024]{1,0:T(8,128)(2,1)}, u32[]{:S(2)}) copy-start(bf16[640,1024]{1,0:T(8,128)(2,1)} %get-tuple-element.37) | copy-start | bytes 3932164
  297.9 254.3 %all-to-all-start = ((bf16[4,2,81920]{2,1,0:T(2,128)(2,1)}), bf16[4,2,81920]{2,1,0:T(2,128)(2,1)}, u32[]{:S(2)}, u32[]{:S(2)}) async-start(bf16[4,2,81920]{2,1,0:T(2,128)(2,1)} %reshape.273), calls=%async_computation | async-start | bytes 2621440 | tf_op jit(solution)/shard_map/all_to_all | solution.py:862
  302.2 338.1 %all-reduce.5.cloned.1.call-start = ((), (), s32[]{:S(2)}) async-start(), calls=%async_computation.10 | async-start | bytes 6291456 | tf_op jit(solution)/shard_map/psum | solution.py:888
  320.0 1.7 copy-start.4
  323.7 210.3 %copy-start.9 = (f32[1,4096]{1,0:T(1,128)S(1)}, f32[1,4096]{1,0:T(1,128)}, u32[]{:S(2)}) copy-start(f32[1,4096]{1,0:T(1,128)} %get-tuple-element.39) | copy-start | bytes 49156
  533.5 73.0 %copy-start.16 = (f32[16]{0:T(128)}, f32[16]{0:T(128)S(1)}, u32[]{:S(2)}) copy-start(f32[16]{0:T(128)S(1)} %pmax.7) | copy-start | bytes 196
  538.2 13.4 %copy-start.15 = (u32[32]{0:T(128)S(1)}, u32[32]{0:T(128)}, u32[]{:S(2)}) copy-start(u32[32]{0:T(128)} %constant.53) | copy-start | bytes 388
  538.2 14.0 %copy-start.10 = (f32[8,1024]{1,0:T(8,128)S(1)}, f32[8,1024]{1,0:T(8,128)}, u32[]{:S(2)}) copy-start(f32[8,1024]{1,0:T(8,128)} %get-tuple-element.38) | copy-start | bytes 98308
  547.6 59.1 %copy-start.13 = (bf16[256]{0:T(256)(128)(2,1)S(1)}, bf16[256]{0:T(256)(128)(2,1)}, u32[]{:S(2)}) copy-start(bf16[256]{0:T(256)(128)(2,1)} %param.22) | copy-start | bytes 1540
  547.6 60.2 %copy-start.3 = (bf16[128,3072]{1,0:T(8,128)(2,1)S(1)}, bf16[128,3072]{1,0:T(8,128)(2,1)}, u32[]{:S(2)}) copy-start(bf16[128,3072]{1,0:T(8,128)(2,1)} %wq_in.1) | copy-start | bytes 2359300
  552.2 71.8 %all-to-all-start.1 = ((bf16[4,2,81920]{2,1,0:T(2,128)(2,1)}), bf16[4,2,81920]{2,1,0:T(2,128)(2,1)}, u32[]{:S(2)}, u32[]{:S(2)}) async-start(bf16[4,2,81920]{2,1,0:T(2,128)(2,1)} %reshape.275), calls=%async_computation.1 | async-start | bytes 2621440 | tf_op jit(solution)/shard_map/all_to_all | solution.py:862
  640.3 4.4 copy-start.7
  642.2 4.1 copy-start.6
Sparse Core Ops, SparseCore 0:
  156.0 39.4 reduce-scatter.6
  279.4 59.8 reduce-scatter.4
  342.8 71.2 reduce-scatter.8
  417.8 71.2 reduce-scatter.10
  491.5 148.7 all-reduce.4
